TPU v7x, 512 devices: a whole 4x4x16 slice. The times are simulated.
512 devices in a mesh: row: 32 (over x_lo, z), col: 8 (over y, core), rep: 2 (over x_hi).
Axes of the slice: x: 4 (x_hi: 2, x_lo: 2; x = x_hi * 2 + x_lo), y: 4, z: 16, core: 2. Of those that a mesh axis runs over, the one named last changes fastest.
Arguments:
- adj_tiles: float32 [32, 8, 4, 512, 512], P('row', 'col'), may hold values from -0.25 to 0.25
- tile_rows: int32 [32, 8, 4], P('row', 'col'), may hold values from 0 to 7
- tile_cols: int32 [32, 8, 4], P('row', 'col'), may hold values from 0 to 31
- tile_counts: int32 [32, 8], P('row', 'col'), may hold values from 1 to 4, as said below
- features_t: float32 [128, 131072], P('rep', ('row', 'col')), may hold values from -6 to 6
- weight: float32 [128, 128], P('rep'), may hold values from -0.5 to 0.5
- bias_vec: float32 [128], replicated, may hold values from -3 to 3
- cotangent: float32 [131072, 128], P(('row', 'col', 'rep')), may hold values from -0.02 to 0.02
Outputs:
- output: float32 [131072, 128], P(('row', 'col', 'rep'))
- grad_weight: float32 [128, 128], P('rep')
- grad_bias: float32 [128], replicated
Inputs may be any that keep to these rules, and one draw needn't show every extreme that they name: `tile_counts`: the number of live slots of each cell; some cell has all 4 slots live. `tile_rows`: block row of a slot inside its row group; dead slots hold arbitrary values. `tile_cols`: block column of a slot inside its column group; dead slots hold arbitrary values.
All inputs are finite; a program needn't handle non-finite values.
Results may differ from a plain program's by a relative error of at most 0.0001.
Values sent between devices are 32-bit elements; how exact they have to be, the bound alone decides.
A program may use at most 64 MiB of HBM per device.

v0:
```python
import functools

import jax
import jax.numpy as jnp
from jax import lax
from jax.sharding import Mesh
from jax.sharding import PartitionSpec as P

COL = ("col_0", "col_1")
ROW = ("row_0", "row_1")
ROW_COL = ("row_0", "row_1", "col_0", "col_1")
ROW_COL_REP = ("row_0", "row_1", "col_0", "col_1", "rep")


def laid_out(pieces, dim):
    pieces = jnp.moveaxis(pieces, 0, dim)
    dims = pieces.shape
    return pieces.reshape(*dims[:dim], dims[dim] * dims[dim + 1], *dims[dim + 2 :])


def stacked_from(array, axes, order):
    pieces = array[None]
    for k in order:
        pieces = lax.all_gather(pieces, axes[k], axis=0, tiled=True)
    current = [lax.axis_size(axes[k]) for k in reversed(order)]
    pieces = pieces.reshape(*current, *array.shape)
    turned = sorted(range(len(order)), key=lambda place: order[len(order) - 1 - place])
    return pieces.transpose(*turned, *range(len(order), pieces.ndim)).reshape(-1, *array.shape)


def whole_of(array, axes, order, dim):
    return laid_out(stacked_from(array, axes, order), dim)


def in_blocks(array, dim, length):
    dims = array.shape
    pieces = array.reshape(*dims[:dim], length, dims[dim] // length, *dims[dim + 1 :])
    return jnp.moveaxis(pieces, dim, 0)


def sent_and_summed(array, axis, dim):
    length = lax.axis_size(axis)
    pieces = lax.all_to_all(in_blocks(array, dim, length), axis, 0, 0, tiled=True)
    return jnp.sum(pieces, axis=0)


def from_everyone(array, axis):
    length = lax.axis_size(axis)
    return lax.all_to_all(
        jnp.broadcast_to(array[None], (length, *array.shape)), axis, 0, 0, tiled=True
    )


def gather_directly(array, axis, dim):
    return laid_out(from_everyone(array, axis), dim)


def over_axes_2(array, axes):
    return functools.reduce(lax.psum, axes, array)


def local(adj_tiles, tile_rows, tile_cols, tile_counts, features_t, weight, bias_vec, cotangent):
    slabs = adj_tiles[0, 0]
    rows_here = tile_rows[0, 0]
    cols_here = tile_cols[0, 0]
    live_count = tile_counts[0, 0]
    slot_count = slabs.shape[0]
    block_len = slabs.shape[1]
    half_width = features_t.shape[0]
    groups = lax.axis_size(COL)
    is_live = jnp.arange(slot_count, dtype=jnp.int32) < live_count
    start_slots = jnp.zeros((slot_count, half_width, block_len), jnp.float32)
    running = start_slots
    shard_piece = whole_of(features_t, ROW, (0, 1), 1)
    span = shard_piece.shape[1]
    for slot_idx in range(slot_count):
        offset_col = cols_here[slot_idx] * block_len
        usable = is_live[slot_idx] & (offset_col >= 0) & (offset_col < span)
        begin_col = jnp.clip(offset_col, 0, span - block_len)

        def add_block(current, slot_idx=slot_idx, begin_col=begin_col):
            columns = lax.dynamic_slice_in_dim(shard_piece, begin_col, block_len, 1)
            product = lax.dot_general(
                columns,
                slabs[slot_idx],
                (((1,), (1,)), ((), ())),
                precision=lax.Precision.HIGHEST,
                preferred_element_type=jnp.float32,
            )
            return current.at[slot_idx].add(product)

        def keep_block(current):
            return current

        running = lax.cond(usable, add_block, keep_block, running)
    placing = (
        (rows_here[:, None] == jnp.arange(groups, dtype=jnp.int32)[None, :]) & is_live[:, None]
    ).astype(jnp.float32)
    mixed_t = jnp.einsum("tg,tfb->fgb", placing, running, precision=lax.Precision.HIGHEST).reshape(
        half_width, groups * block_len
    )
    own_block = sent_and_summed(mixed_t, COL, 1)
    local_rows = lax.dot_general(
        own_block,
        weight,
        (((0,), (0,)), ((), ())),
        precision=lax.Precision.HIGHEST,
        preferred_element_type=jnp.float32,
    )
    preact = sent_and_summed(local_rows, "rep", 0)
    repeats = 1
    preact = preact + bias_vec
    squash = jax.nn.sigmoid(preact)
    output = preact * squash
    slope = cotangent * squash * (1.0 + preact * (1.0 - squash))
    contract_shard_piece = gather_directly(slope, "rep", 0)
    grad_part = jnp.dot(
        own_block,
        contract_shard_piece,
        precision=lax.Precision.HIGHEST,
        preferred_element_type=jnp.float32,
    )
    local_bias = jnp.sum(contract_shard_piece, axis=0)
    grad_weight, summed_bias = (over_axes_2(grad_part, ROW_COL), over_axes_2(local_bias, ROW_COL))
    grad_bias = summed_bias / repeats
    return (output, grad_weight, grad_bias)


def solution(mesh):
    split = Mesh(
        mesh.devices.reshape(2, 16, 4, 2, mesh.shape["rep"]),
        ("row_0", "row_1", "col_0", "col_1", "rep"),
    )
    return jax.shard_map(
        local,
        mesh=split,
        in_specs=(
            P(ROW, COL, None, None, None),
            P(ROW, COL, None),
            P(ROW, COL, None),
            P(ROW, COL),
            P("rep", ROW_COL),
            P("rep", None),
            P(),
            P(ROW_COL_REP, None),
        ),
        out_specs=(P(ROW_COL_REP, None), P("rep", None), P()),
        check_vma=False,
    )
```

profile of v0, /device:TPU:1, one launch (start us, length us, event | category | flops | bytes accessed | tf_op | source)
XLA Modules:
  0.0 246.7 jit_solution(15389885308639466295)
XLA Ops:
  7.2 0.0 copy-start
  7.2 0.0 all-gather.3.cloned.1.call-start
  7.2 6.9 %all-gather = f32[128,512]{1,0:T(8,128)} all-gather(f32[64,512]{1,0:T(8,128)} %param.28), channel_id=2, replica_groups=mesh['row_0'=2,'row_1'=16,'col_0'=4,'col_1'=2,'rep'=2] {'row_0'}, dimensions={0}, use_global_device_ids=true | all-gather | bytes 393216 | tf_op jit(solution)/shard_map/all_gather | solution.py:24
  14.1 0.0 all-gather.3.cloned.1.call-update
  14.2 1.4 fusion.33
  18.8 0.7 fusion.34
  22.1 67.1 %all-gather.3.cloned.1.call-done = f32[32,64,512]{2,1,0:T(8,128)} async-done(((f32[2,64,512]{2,1,0:T(8,128)}), f32[32,64,512]{2,1,0:T(8,128)}) %all-gather.3.cloned.1.call-update) | async-done | bytes 4194320 | tf_op jit(solution)/shard_map/all_gather | solution.py:24
  89.2 2.8 %copy.27 = f32[2,16,64,512]{3,2,1,0:T(8,128)S(1)} copy(f32[2,16,64,512]{3,2,0,1:T(8,128)} %bitcast.83) | data formatting | bytes 8388608 | tf_op jit(solution)/shard_map/transpose | solution.py:28
  91.9 2.6 %copy.35 = f32[32,8,8,512]{3,2,0,1:T(8,128)} copy(f32[32,8,8,512]{3,2,1,0:T(8,128)S(1)} %bitcast.74) | data formatting | bytes 8388608 | tf_op jit(solution)/shard_map/reshape | solution.py:18
  94.5 0.0 copy-start.2
  94.5 2.5 %conditional.4 = (f32[4,64,512]{2,1,0:T(8,128)S(1)}) conditional(s32[]{:T(128)} %convert_element_type.16, () %tuple.48, (s32[1,1,1]{2,1,0:T(1,128)}, f32[64,16384]{1,0:T(8,128)}, f32[4,512,512]{2,1,0:T(8,128)}, s32[1,1,1]{2,1,0:T(1,128)}, s32[1,1,1]{2,1,0:T(1,128)}) %tuple.77), branch_computations={%region_0.1_spmd, %region_1.2_spmd} | conditional | flops 201326592 | bytes 1966154 | solution.py:95
  94.5 2.4 convolution_bitcast_fusion
  97.0 0.1 scatter-add.6
  97.0 2.5 %conditional.5 = (f32[4,64,512]{2,1,0:T(8,128)S(1)}) conditional(s32[]{:T(128)} %convert_element_type.15, f32[4,64,512]{2,1,0:T(8,128)S(1)} %get-tuple-element.151, (f32[4,64,512]{2,1,0:T(8,128)S(1)}, s32[1,1,1]{2,1,0:T(1,128)}, f32[64,16384]{1,0:T(8,128)}, f32[4,512,512]{2,1,0:T(8,128)}, s32[1,1,1]{2,1,0:T(1,128)}, ...), branch_computations={%region_2.0_spmd, %region_3.4_spmd} | conditional | flops 201359360 | bytes 1441862 | solution.py:95
  97.0 2.5 fusion.5
  99.5 2.5 %conditional.6 = (f32[4,64,512]{2,1,0:T(8,128)S(1)}) conditional(s32[]{:T(128)} %convert_element_type.14, f32[4,64,512]{2,1,0:T(8,128)S(1)} %get-tuple-element.152, (f32[4,64,512]{2,1,0:T(8,128)S(1)}, s32[1,1,1]{2,1,0:T(1,128)}, f32[64,16384]{1,0:T(8,128)}, f32[4,512,512]{2,1,0:T(8,128)}, s32[1,1,1]{2,1,0:T(1,128)}, ...), branch_computations={%region_4.5_spmd, %region_5.0_spmd} | conditional | flops 201359360 | bytes 1441862 | solution.py:95
  99.5 2.5 fusion.11
  102.0 0.4 conditional.7
  102.0 0.3 copy.32
  102.4 0.0 copy-start.1
  102.4 0.0 copy-start.3
  102.4 0.0 copy-done.2
  102.4 0.8 fusion.29
  103.2 0.6 copy.30
  103.8 28.4 %all_to_all.15 = f32[8,64,512]{2,1,0:T(8,128)S(1)} all-to-all(f32[8,64,512]{2,1,0:T(8,128)S(1)} %copy.30), channel_id=1, replica_groups=mesh['row_0'=2,'row_1'=16,'col_0'=4,'col_1'=2,'rep'=2] {'col_0','col_1'}, dimensions={0} | all-to-all | bytes 2097152 | tf_op jit(solution)/shard_map/all_to_all | solution.py:43
  132.2 0.1 reduce_sum.27
  132.3 0.0 copy-done
  132.3 0.6 fusion.22
  132.9 9.3 %all_to_all.16 = f32[2,256,128]{2,1,0:T(8,128)S(1)} all-to-all(f32[2,256,128]{2,1,0:T(8,128)S(1)} %fusion.22), channel_id=1, replica_groups=mesh['row_0'=2,'row_1'=16,'col_0'=4,'col_1'=2,'rep'=2] {'rep'}, dimensions={0} | all-to-all | bytes 524288 | tf_op jit(solution)/shard_map/all_to_all | solution.py:43
  142.2 0.0 copy-done.1
  142.2 0.0 copy-done.3
  142.3 0.7 add_multiply_fusion
  143.0 7.9 %all_to_all.17 = f32[2,256,128]{2,1,0:T(8,128)S(1)} all-to-all(f32[2,256,128]{2,1,0:T(8,128)S(1)} %broadcast_in_dim.9), channel_id=1, replica_groups=mesh['row_0'=2,'row_1'=16,'col_0'=4,'col_1'=2,'rep'=2] {'rep'}, dimensions={0} | all-to-all | bytes 524288 | tf_op jit(solution)/shard_map/all_to_all | solution.py:49
  150.9 0.3 fusion.35
  151.2 0.1 reduce_sum.29
  151.3 5.5 %all-reduce.4 = (f32[64,128]{1,0:T(8,128)S(1)}, f32[128]{0:T(128)S(1)}) all-reduce(f32[64,128]{1,0:T(8,128)S(1)} %fusion.35, f32[128]{0:T(128)S(1)} %reduce_sum.29), channel_id=1, replica_groups=mesh['row_0'=2,'row_1'=16,'col_0'=4,'col_1'=2,'rep'=2] {'row_0'}, use_global_device_ids=true, to_apply=%region_10.11 | all-reduce | flops 8320 | bytes 66560 | tf_op jit(solution)/shard_map/psum | solution.py:59
  156.8 43.8 %all-reduce.1 = (f32[64,128]{1,0:T(8,128)S(1)}, f32[128]{0:T(128)S(1)}) all-reduce(f32[64,128]{1,0:T(8,128)S(1)} %get-tuple-element.137, f32[128]{0:T(128)S(1)} %get-tuple-element.138), channel_id=1, replica_groups=mesh['row_0'=2,'row_1'=16,'col_0'=4,'col_1'=2,'rep'=2] {'row_1'}, use_global_device_ids=true, to_apply=%region_11.0 | all-reduce | flops 8320 | bytes 66560 | tf_op jit(solution)/shard_map/psum | solution.py:59
  200.6 12.0 %all-reduce.2 = (f32[64,128]{1,0:T(8,128)S(1)}, f32[128]{0:T(128)S(1)}) all-reduce(f32[64,128]{1,0:T(8,128)S(1)} %get-tuple-element.131, f32[128]{0:T(128)S(1)} %get-tuple-element.132), channel_id=1, replica_groups=mesh['row_0'=2,'row_1'=16,'col_0'=4,'col_1'=2,'rep'=2] {'col_0'}, use_global_device_ids=true, to_apply=%region_12.13 | all-reduce | flops 8320 | bytes 66560 | tf_op jit(solution)/shard_map/psum | solution.py:59
  212.6 27.2 %all-reduce.3 = (f32[64,128]{1,0:T(8,128)}, f32[128]{0:T(128)}) all-reduce(f32[64,128]{1,0:T(8,128)S(1)} %get-tuple-element.133, f32[128]{0:T(128)S(1)} %get-tuple-element.134), channel_id=1, replica_groups=mesh['row_0'=2,'row_1'=16,'col_0'=4,'col_1'=2,'rep'=2] {'col_1'}, use_global_device_ids=true, to_apply=%region_13.14 | all-reduce | flops 8320 | bytes 66560 | tf_op jit(solution)/shard_map/psum | solution.py:59
  (3 shorter events, 0.0 us)
Async XLA Ops:
  7.2 125.1 %copy-start = (f32[64,128]{1,0:T(8,128)S(1)}, f32[64,128]{1,0:T(8,128)}, u32[]{:S(2)}) copy-start(f32[64,128]{1,0:T(8,128)} %param.29) | copy-start | bytes 98308
  7.2 82.0 %all-gather.3.cloned.1.call-start = ((), (), s32[]{:S(2)}) async-start(), calls=%async_computation.3 | async-start | bytes 4456448 | tf_op jit(solution)/shard_map/all_gather | solution.py:24
  94.5 7.9 %copy-start.2 = (s32[1,1,4]{2,1,0:T(1,128)S(1)}, s32[1,1,4]{2,1,0:T(1,128)}, u32[]{:S(2)}) copy-start(s32[1,1,4]{2,1,0:T(1,128)} %param.25) | copy-start | bytes 52
  102.4 39.9 %copy-start.1 = (f32[256,128]{1,0:T(8,128)S(1)}, f32[256,128]{1,0:T(8,128)}, u32[]{:S(2)}) copy-start(f32[256,128]{1,0:T(8,128)} %param.31) | copy-start | bytes 393220
  102.4 39.9 %copy-start.3 = (f32[128]{0:T(128)S(1)}, f32[128]{0:T(128)}, u32[]{:S(2)}) copy-start(f32[128]{0:T(128)} %param.30) | copy-start | bytes 1540
Sparse Core Ops, SparseCore 0:
  14.3 74.8 all-gather.2
where the time goes:
time: 246 us; the launch traced here: 247 us
  blocking collectives  141 us (57%)
  waiting for transfers between devices  67.1 us (27%)
  between operations  20.1 us (8%)
  matrix products  9.02 us (4%)
  local copies, waits for them, and re-layouts  8.42 us (3%)
    psum x4, blocking collectives, over_axes_2(): return functools.reduce(lax.psum, axes, array)  88.5 us
    all_gather x1, waiting for transfers between devices, stacked_from(): pieces = lax.all_gather(pieces, axes[k], axis=0, tiled=True)  67.1 us
    all_to_all x2, blocking collectives, sent_and_summed(): lax.all_to_all(in_blocks(array, dim, length), axis, 0, 0, tiled=True)  37.7 us
    all_to_all x1, blocking collectives, from_everyone(): lax.all_to_all(jnp.broadcast_to(array[None], (length, *array.shape)), axi...  7.92 us
    dot_general x3, matrix products, add_block(): lax.dot_general(columns, slabs[slot_idx], (((1,), (1,)), ((), ())), preci...  7.38 us
    all_gather x1, blocking collectives, stacked_from(): pieces = lax.all_gather(pieces, axes[k], axis=0, tiled=True)  6.9 us
  transfers between devices with their start and end apart: 1, of which 1 were waited for; matrix products, arithmetic and copies ran while one was open for 1% of the time, Pallas kernels for 0%

commit v1 on v0

v1 whole, which is shorter than its diff:
```python
import functools

import jax
import jax.numpy as jnp
from jax import lax
from jax.experimental import pallas as pl
from jax.experimental.pallas import tpu as pltpu
from jax.sharding import PartitionSpec as P

MESH = pl.DeviceIdType.MESH
F32 = jnp.float32
BF16 = jnp.bfloat16
HIGHEST = lax.Precision.HIGHEST

NY = 4
CHIPS = 16
OVER_X = 40
OFFSETS = (2, 1, 3, 0)


def remote(src, dst, send_sem, recv_sem, device):
    return pltpu.make_async_remote_copy(
        src_ref=src, dst_ref=dst, send_sem=send_sem, recv_sem=recv_sem, device_id=device, device_id_type=MESH
    )


def kernel(
    nz,
    rows_ref, cols_ref, counts_ref, adj_ref, feat_ref, weight_ref, bias_ref, cot_ref,
    out_ref, gw_ref, gb_ref,
    gath, adj_in, adj_hi, adj_lo, prod, m_out, c1_in, s_buf,
    relay, direct, mid, final, away, mt, w_full, cot, out_v,
    g_buf, f1_in, f2_in, f3_in, p2, p3, b_one, b_two, b1_in, b2_in, b3_in,
    zr, xr, xo, zs, xs, lsem, asem, wsem, csem, ysem, ysend, dsem, fsem,
):
    row, col, rep = lax.axis_index("row"), lax.axis_index("col"), lax.axis_index("rep")
    x_lo, z = row // nz, row % nz
    y, core = col // 2, col % 2
    far = nz // 2
    width, block = feat_ref.shape
    half_w, half_b = width // 2, block // 2
    keep = width - OVER_X

    z_dev = ({"row": x_lo * nz + (z + 1) % nz}, {"row": x_lo * nz + (z + nz - 1) % nz})
    x_dev = {"row": (1 - x_lo) * nz + z}
    core_dev = {"col": y * 2 + 1 - core}
    y_dev = ({"col": ((y + 1) % NY) * 2 + core}, {"col": ((y + NY - 1) % NY) * 2 + core})
    rep_dev = {"rep": 1 - rep}

    barrier = pltpu.get_barrier_semaphore()
    for device in (*z_dev, x_dev, core_dev, *y_dev, rep_dev):
        pl.semaphore_signal(barrier, inc=1, device_id=device, device_id_type=MESH)

    adj_copies = [pltpu.make_async_copy(adj_ref.at[0, 0, t], adj_in.at[t], asem.at[t]) for t in range(4)]
    own_copy = pltpu.make_async_copy(feat_ref, gath.at[row], lsem.at[0])
    cot_copy = pltpu.make_async_copy(cot_ref, cot, lsem.at[1])
    w_copy = pltpu.make_async_copy(weight_ref, w_full.at[pl.ds(rep * width, width)], lsem.at[2])

    pl.semaphore_wait(barrier, 7)

    def slot(plane, hops, way):
        return plane * nz + (z + nz - hops if way == 0 else z + hops) % nz

    def over_z(plane, hops, way, low, count, part, first=False):
        place = slot(plane, hops - 1, way)
        source = feat_ref if first else gath.at[place]
        return remote(
            source.at[pl.ds(low, count)],
            gath.at[place, pl.ds(low, count)],
            zs.at[0 if part < 2 else (1 if hops < far else 2)],
            zr.at[way, hops - 1, part],
            z_dev[way],
        )

    def landed_z(plane, hops, way, low, count, part):
        place = gath.at[slot(plane, hops, way), pl.ds(low, count)]
        remote(place, place, zs.at[0], zr.at[way, hops - 1, part], z_dev[way]).wait_recv()

    def over_x(hops, way):
        piece = gath.at[slot(x_lo, hops, way), pl.ds(0, OVER_X)]
        return remote(piece, piece, xs.at[1], xr.at[way, hops - 1], x_dev)

    def landed_x(hops, way):
        piece = gath.at[slot(1 - x_lo, hops, way), pl.ds(0, OVER_X)]
        remote(piece, piece, xs.at[1], xr.at[way, hops - 1], x_dev).wait_recv()

    def own_over_x(low, count, which, place):
        return remote(
            feat_ref.at[pl.ds(low, count)], gath.at[place, pl.ds(low, count)], xs.at[0], xo.at[which], x_dev
        )

    own_over_x(OVER_X, keep, 1, row).start()
    for way in (0, 1):
        over_z(x_lo, 1, way, 0, OVER_X, 0, True).start()
    for way in (0, 1):
        over_z(x_lo, 1, way, OVER_X, keep, 1, True).start()
    own_over_x(0, OVER_X, 0, row).start()
    for copy in (own_copy, *adj_copies, cot_copy, w_copy):
        copy.start()
    w_send = remote(weight_ref, w_full.at[pl.ds(rep * width, width)], wsem.at[0], wsem.at[1], rep_dev)
    w_send.start()

    chunk = 32
    chunks = block // chunk * 4

    def split(first, count):
        def one(i, carry):
            t, low = i // (block // chunk), pl.multiple_of((i % (block // chunk)) * chunk, chunk)
            value = adj_in[t, pl.ds(low, chunk), :]
            high = value.astype(BF16)
            adj_hi[t, pl.ds(low, chunk), :] = high
            adj_lo[t, pl.ds(low, chunk), :] = (value - high.astype(F32)).astype(BF16)
            return carry

        lax.fori_loop(first, first + count, one, 0)

    partner = (1 - x_lo) * nz + z
    own_over_x(OVER_X, keep, 1, partner).wait_recv()
    for way in (0, 1):
        over_z(1 - x_lo, 1, way, OVER_X, keep, 2).start()
    done = 0
    for hops in range(1, far):
        last = hops == far - 1
        for way in (0, 1):
            landed_z(x_lo, hops, way, 0, OVER_X, 0)
            if not last:
                over_z(x_lo, hops + 1, way, 0, OVER_X, 0).start()
            over_x(hops, way).start()
            if last and way == 0:
                over_z(x_lo, far, 0, 0, half_w, 0).start()
        for way in (0, 1):
            landed_z(x_lo, hops, way, OVER_X, keep, 1)
            if not last:
                over_z(x_lo, hops + 1, way, OVER_X, keep, 1).start()
            elif way == 1:
                over_z(x_lo, far, 1, half_w, half_w, 0).start()
        for way in (0, 1):
            landed_z(1 - x_lo, hops, way, OVER_X, keep, 2)
            if not last:
                over_z(1 - x_lo, hops + 1, way, OVER_X, keep, 2).start()
        if last:
            for way in (0, 1):
                landed_x(hops, way)
                over_z(1 - x_lo, far, way, way * half_w, half_w, 2).start()
        if hops == 1:
            for copy in adj_copies:
                copy.wait()
        upto = chunks * hops // (far - 1)
        split(done, upto - done)
        done = upto
    own_over_x(0, OVER_X, 0, partner).wait_recv()
    for hops in range(1, far - 1):
        for way in (0, 1):
            landed_x(hops, way)
    for copy in (own_copy, cot_copy, w_copy):
        copy.wait()
    for way in (0, 1):
        landed_z(x_lo, far, way, way * half_w, half_w, 0)
        landed_z(1 - x_lo, far, way, way * half_w, half_w, 2)

    count = counts_ref[0, 0]
    for t in range(4):
        value = gath[jnp.clip(cols_ref[0, 0, t], 0, 2 * nz - 1)]
        high = value.astype(BF16)
        low = (value - high.astype(F32)).astype(BF16)
        dims = (((1,), (1,)), ((), ()))
        both = lax.dot_general(jnp.concatenate([high, low], axis=0), adj_hi[t], dims, preferred_element_type=F32)
        rest = lax.dot_general(high, adj_lo[t], dims, preferred_element_type=F32)
        prod[t] = both[:width] + both[width:] + rest

    def placed(group):
        total = None
        for t in range(4):
            scale = jnp.where((t < count) & (rows_ref[0, 0, t] == group), F32(1.0), F32(0.0))
            term = prod[t] * scale
            total = term if total is None else total + term
        return total

    core_copies = []
    for k, offset in enumerate(OFFSETS):
        total = placed(((y + offset) % NY) * 2 + 1 - core)
        for h in (0, 1):
            m_out[k, h] = total[:, h * half_b : (h + 1) * half_b]
        copy = remote(m_out.at[k], c1_in.at[k], csem.at[0, k], csem.at[1, k], core_dev)
        copy.start()
        core_copies.append(copy)
    order = ((0, 1 - rep), (1, rep))
    up, down = pl.ds(0, half_w), pl.ds(half_w, half_w)
    y_copies = {}

    def over_y(src, dst, name, n, way):
        index = ("relay0", "relay1", "direct0", "direct1", "final0", "final1").index(name) * 2 + n
        copy = remote(src, dst, ysend.at[index], ysem.at[index], y_dev[way])
        copy.start()
        y_copies[name, n] = copy

    for k, offset in enumerate(OFFSETS):
        total = placed(((y + offset) % NY) * 2 + core)
        core_copies[k].wait_recv()
        for h in (0, 1):
            s_buf[k, h] = total[:, h * half_b : (h + 1) * half_b] + c1_in[k, h]
        for n, h in order:
            if offset == 2:
                over_y(s_buf.at[k, h, up], relay.at[0, n], "relay0", n, 0)
                over_y(s_buf.at[k, h, down], relay.at[1, n], "relay1", n, 1)
            elif offset == 1:
                over_y(s_buf.at[k, h, down], direct.at[1, n], "direct1", n, 0)
            elif offset == 3:
                over_y(s_buf.at[k, h, up], direct.at[0, n], "direct0", n, 1)
    for n, h in order:
        y_copies["relay0", n].wait_recv()
        mid[0, n] = relay[0, n] + s_buf[1, h, up]
        over_y(mid.at[0, n], final.at[0, n], "final0", n, 0)
        y_copies["relay1", n].wait_recv()
        mid[1, n] = relay[1, n] + s_buf[2, h, down]
        over_y(mid.at[1, n], final.at[1, n], "final1", n, 1)
    away_copy = remote(away, mt.at[pl.ds(rep * width, width)], dsem.at[0], dsem.at[1], rep_dev)
    for n, h in order:
        for part in (0, 1):
            y_copies["direct%d" % part, n].wait_recv()
            y_copies["final%d" % part, n].wait_recv()
            rows = pl.ds(part * half_w, half_w)
            total = s_buf[3, h, rows] + final[part, n] + direct[part, n]
            if n == 0:
                away[rows] = total
            else:
                mt[pl.ds(pl.multiple_of(rep * width + part * half_w, half_w), half_w), :] = total
        if n == 0:
            away_copy.start()
    w_send.wait_recv()
    away_copy.wait_recv()

    preact = jnp.dot(mt[...].T, w_full[...], precision=HIGHEST, preferred_element_type=F32) + bias_ref[...]
    squash = 1.0 / (1.0 + jnp.exp(-preact))
    out_v[...] = preact * squash
    out_copy = pltpu.make_async_copy(out_v, out_ref, lsem.at[3])
    out_copy.start()
    slope = cot[...] * squash * (1.0 + preact * (1.0 - squash))
    grad = jnp.dot(mt[...], slope, precision=HIGHEST, preferred_element_type=F32)
    g_buf[...] = grad.reshape(CHIPS, 8, 128)
    b_one[...] = jnp.sum(slope, axis=0, keepdims=True)

    me = rep * 8 + x_lo * 4 + y
    f1 = []
    for j in range(1, CHIPS):
        peer = (me + j) % CHIPS
        device = {"row": ((peer // 4) % 2) * nz + z, "col": (peer % 4) * 2 + core, "rep": peer // 8}
        f1.append(remote(g_buf.at[peer], f1_in.at[j - 1], fsem.at[0], fsem.at[1], device))
        f1.append(remote(b_one, b1_in.at[j - 1], fsem.at[2], fsem.at[3], device))
    for copy in f1:
        copy.start()
    remote(f1_in, f1_in, fsem.at[0], fsem.at[1], rep_dev).wait_recv()
    remote(b1_in, b1_in, fsem.at[2], fsem.at[3], rep_dev).wait_recv()
    mine = jnp.sum(f1_in[...], axis=0) + g_buf[me]
    bias_sum = jnp.sum(b1_in[...], axis=0) + b_one[...]
    p2[...] = mine
    f2_in[z] = mine
    b_two[...] = bias_sum
    b2_in[z] = bias_sum
    for k in sorted(range(1, nz), key=lambda j: -min(j, nz - j)):
        device = {"row": x_lo * nz + (z + k) % nz}
        remote(p2, f2_in.at[z], fsem.at[4], fsem.at[5], device).start()
        remote(b_two, b2_in.at[z], fsem.at[6], fsem.at[7], device).start()
    others = pl.ds(0, nz - 1)
    remote(f2_in.at[others], f2_in.at[others], fsem.at[4], fsem.at[5], rep_dev).wait()
    remote(b2_in.at[others], b2_in.at[others], fsem.at[6], fsem.at[7], rep_dev).wait()
    mine = jnp.sum(f2_in[...], axis=0)
    bias_sum = jnp.sum(b2_in[...], axis=0)
    p3[...] = mine
    place = x_lo * 4 + y
    f3_in[core, place] = mine
    b_two[...] = bias_sum
    b3_in[core] = bias_sum
    here = core * 8 + place
    for j in range(1, 16):
        peer = (here + j) % 16
        device = {"row": ((peer // 4) % 2) * nz + z, "col": (peer % 4) * 2 + peer // 8}
        remote(p3, f3_in.at[core, place], fsem.at[8], fsem.at[9], device).start()
    b3 = remote(b_two, b3_in.at[core], fsem.at[10], fsem.at[11], core_dev)
    b3.start()
    remote(f1_in, f1_in, fsem.at[8], fsem.at[9], rep_dev).wait()
    b3.wait()
    gw_ref[...] = (f3_in[0] + f3_in[1]).reshape(width, 128)
    gb_ref[...] = b3_in[0] + b3_in[1]

    out_copy.wait()
    remote(gath.at[pl.ds(0, nz - 1)], gath.at[pl.ds(0, nz - 1)], zs.at[0], zr.at[0, 0, 0], rep_dev).wait_send()
    part = gath.at[pl.ds(0, nz - 2), pl.ds(0, keep)]
    remote(part, part, zs.at[1], zr.at[0, 0, 0], rep_dev).wait_send()
    remote(gath.at[0], gath.at[0], zs.at[2], zr.at[0, 0, 0], rep_dev).wait_send()
    remote(gath.at[0], gath.at[0], xs.at[0], xr.at[0, 0], rep_dev).wait_send()
    part = gath.at[pl.ds(0, nz - 2), pl.ds(0, OVER_X)]
    remote(part, part, xs.at[1], xr.at[0, 0], rep_dev).wait_send()
    w_send.wait_send()
    away_copy.wait_send()
    for copy in (*core_copies, *y_copies.values()):
        copy.wait_send()
    remote(f1_in, f1_in, fsem.at[0], fsem.at[1], rep_dev).wait_send()
    remote(b1_in, b1_in, fsem.at[2], fsem.at[3], rep_dev).wait_send()


def solution(mesh):
    nz = mesh.shape["row"] // 2

    def local(adj_tiles, tile_rows, tile_cols, tile_counts, features_t, weight, bias_vec, cotangent):
        width, block = features_t.shape
        half_w, half_b = width // 2, block // 2
        out_w = weight.shape[1]
        nodes = cotangent.shape[0]
        smem = pl.BlockSpec(memory_space=pltpu.SMEM)
        vmem = pl.BlockSpec(memory_space=pltpu.VMEM)
        hbm = pl.BlockSpec(memory_space=pl.ANY)
        dma = pltpu.SemaphoreType.DMA
        output, grad_weight, grad_bias = pl.pallas_call(
            functools.partial(kernel, nz),
            out_shape=(
                jax.ShapeDtypeStruct((nodes, out_w), F32),
                jax.ShapeDtypeStruct((width, out_w), F32),
                jax.ShapeDtypeStruct((1, out_w), F32),
            ),
            in_specs=[smem, smem, smem, hbm, hbm, hbm, vmem, hbm],
            out_specs=(hbm, vmem, vmem),
            scratch_shapes=[
                pltpu.VMEM((2 * nz, width, block), F32),
                pltpu.VMEM((4, block, block), F32),
                pltpu.VMEM((4, block, block), BF16),
                pltpu.VMEM((4, block, block), BF16),
                pltpu.VMEM((4, width, block), F32),
                pltpu.VMEM((4, 2, width, half_b), F32),
                pltpu.VMEM((4, 2, width, half_b), F32),
                pltpu.VMEM((4, 2, width, half_b), F32),
                pltpu.VMEM((2, 2, half_w, half_b), F32),
                pltpu.VMEM((2, 2, half_w, half_b), F32),
                pltpu.VMEM((2, 2, half_w, half_b), F32),
                pltpu.VMEM((2, 2, half_w, half_b), F32),
                pltpu.VMEM((width, half_b), F32),
                pltpu.VMEM((2 * width, half_b), F32),
                pltpu.VMEM((2 * width, out_w), F32),
                pltpu.VMEM((nodes, out_w), F32),
                pltpu.VMEM((nodes, out_w), F32),
                pltpu.VMEM((CHIPS, 8, out_w), F32),
                pltpu.VMEM((CHIPS - 1, 8, out_w), F32),
                pltpu.VMEM((nz, 8, out_w), F32),
                pltpu.VMEM((2, 8, 8, out_w), F32),
                pltpu.VMEM((8, out_w), F32),
                pltpu.VMEM((8, out_w), F32),
                pltpu.VMEM((1, out_w), F32),
                pltpu.VMEM((1, out_w), F32),
                pltpu.VMEM((CHIPS - 1, 1, out_w), F32),
                pltpu.VMEM((nz, 1, out_w), F32),
                pltpu.VMEM((2, 1, out_w), F32),
                dma((2, nz // 2, 3)),
                dma((2, nz // 2)),
                dma((2,)),
                dma((3,)),
                dma((2,)),
                dma((4,)),
                dma((4,)),
                dma((2,)),
                dma((2, 4)),
                dma((12,)),
                dma((12,)),
                dma((2,)),
                dma((12,)),
            ],
            compiler_params=pltpu.CompilerParams(
                collective_id=0, has_side_effects=True, vmem_limit_bytes=48 * 1024 * 1024
            ),
        )(tile_rows, tile_cols, tile_counts, adj_tiles, features_t, weight, bias_vec.reshape(1, out_w), cotangent)
        return output, grad_weight, grad_bias.reshape(out_w)

    return jax.shard_map(
        local,
        mesh=mesh,
        in_specs=(
            P("row", "col", None, None, None),
            P("row", "col", None),
            P("row", "col", None),
            P("row", "col"),
            P("rep", ("row", "col")),
            P("rep", None),
            P(),
            P(("row", "col", "rep"), None),
        ),
        out_specs=(P(("row", "col", "rep"), None), P("rep", None), P()),
        check_vma=False,
    )
```

time: 246 us -> 93.2 us (0.38)
  blocking collectives: 141 us -> 0 us
  Pallas kernels: 0 us -> 83.1 us
  waiting for transfers between devices: 67.1 us -> 0 us
  between operations: 20.1 us -> 1.3 us
  matrix products: 9.02 us -> 0 us
    psum x4 -> x0, blocking collectives: 88.5 us -> none  [over_axes_2(): return functools.reduce(lax.psum, axes, array)]
    pallas_call x0 -> x1, Pallas kernels: none -> 83.1 us  [local(): pl.pallas_call(functools.partial(kernel, nz), out_shape=(jax.ShapeDtypeSt...]
    all_gather x1 -> x0, waiting for transfers between devices: 67.1 us -> none  [stacked_from(): pieces = lax.all_gather(pieces, axes[k], axis=0, tiled=True)]
    all_to_all x3 -> x0, blocking collectives: 45.6 us -> none  [the longest x2 37.7 us: sent_and_summed(): lax.all_to_all(in_blocks(array, dim, length), axis, 0, 0, tiled=True)]
    dot_general x6 -> x0, matrix products: 9.02 us -> none  [the longest x3 7.38 us: add_block(): lax.dot_general(columns, slabs[slot_idx], (((1,), (1,)), ((), ())), preci...]
    unnamed x8 -> x17, local copies, waits for them, and re-layouts: 0.03 us -> 8.49 us
    all_gather x1 -> x0, blocking collectives: 6.9 us -> none  [stacked_from(): pieces = lax.all_gather(pieces, axes[k], axis=0, tiled=True)]
    transpose x1 -> x0, local copies, waits for them, and re-layouts: 2.75 us -> none  [stacked_from(): pieces.transpose(*turned, *range(len(order), pieces.ndim))]
  transfers between devices with their start and end apart: 1 -> 0, of which waited for: 1 -> 0; matrix products, arithmetic and copies ran while one was open for 1% -> 0% of each run, Pallas kernels for 0% -> 0%
where the time goes in v1:
time: 93.2 us; the launch traced here: 92.9 us
  Pallas kernels  83.1 us (89%)
  local copies, waits for them, and re-layouts  8.49 us (9%)
  between operations  1.3 us (1%)
    pallas_call x1, Pallas kernels, local(): pl.pallas_call(functools.partial(kernel, nz), out_shape=(jax.ShapeDtypeSt...  83.1 us
    unnamed x17, local copies, waits for them, and re-layouts  8.49 us

profile of v1, /device:TPU:1, one launch (start us, length us, event | category | flops | bytes accessed | tf_op | source)
XLA Modules:
  0.0 92.9 jit_solution(12323636760871467741)
XLA Ops:
  1.3 0.0 copy-start
  1.3 2.2 %copy-done = f32[1,1,4,512,512]{4,3,2,1,0:T(8,128)S(1)} copy-done((f32[1,1,4,512,512]{4,3,2,1,0:T(8,128)S(1)}, f32[1,1,4,512,512]{4,3,2,1,0:T(8,128)}, u32[]{:S(2)}) %copy-start) | copy-done | bytes 4194328
  3.5 0.0 copy-start.1
  3.5 0.9 copy-done.1
  4.4 0.0 copy-start.2
  4.4 0.9 copy-done.2
  5.3 0.0 copy-start.3
  5.3 0.8 copy-done.3
  6.0 0.0 copy-start.4
  6.0 0.7 copy-done.4
  6.7 0.0 copy-start.5
  6.7 0.7 copy-done.5
  7.3 0.0 copy-start.6
  7.3 0.7 copy-done.6
  8.0 83.1 %shard_map.103 = (f32[256,128]{1,0:T(8,128)S(1)}, f32[64,128]{1,0:T(8,128)S(1)}, f32[1,128]{1,0:T(1,128)S(1)}) custom-call(s32[1,1,4]{2,1,0:T(1,128)S(1)} %copy-done.4, s32[1,1,4]{2,1,0:T(1,128)S(1)} %copy-done.5, s32[1,1]{1,0:T(1,128)S(6)} %copy.14.counts_ref, f32[1,1,4,512,512]{4,3,2,1,0:T(8,128)S(1)} %copy-done, f32[64,512]{1,0:T(8,128)S(1)} %copy-done.1, ...), custom_call_target="tpu_custom_call" | custom-call | tf_op jit(solution)/shard_map/pallas_call | solution.py:314
  91.1 0.7 copy.15
  91.8 0.6 copy.16
  92.4 0.5 copy.17
Async XLA Ops:
  1.3 2.2 %copy-start = (f32[1,1,4,512,512]{4,3,2,1,0:T(8,128)S(1)}, f32[1,1,4,512,512]{4,3,2,1,0:T(8,128)}, u32[]{:S(2)}) copy-start(f32[1,1,4,512,512]{4,3,2,1,0:T(8,128)} %adj_ref.1) | copy-start | bytes 12582916
  3.5 0.9 copy-start.1
  4.4 0.9 copy-start.2
  5.3 0.8 copy-start.3
  6.0 0.7 copy-start.4
  6.7 0.7 copy-start.5
  7.3 0.7 copy-start.6

commit v2 on v1

v2 whole, which is shorter than its diff:
```python
import functools

import jax
import jax.numpy as jnp
from jax import lax
from jax.experimental import pallas as pl
from jax.experimental.pallas import tpu as pltpu
from jax.sharding import PartitionSpec as P

MESH = pl.DeviceIdType.MESH
F32 = jnp.float32
BF16 = jnp.bfloat16
HIGHEST = lax.Precision.HIGHEST

NY = 4
PIECES = 32
CHUNK = 16
OWN_ORDER = (2, 0, 1, 3)
OFFSETS = (2, 1, 3, 0)


def remote(src, dst, send_sem, recv_sem, device):
    return pltpu.make_async_remote_copy(
        src_ref=src, dst_ref=dst, send_sem=send_sem, recv_sem=recv_sem, device_id=device, device_id_type=MESH
    )


def kernel(
    nz,
    rows_ref, cols_ref, counts_ref, adj_ref, feat_ref, weight_ref, bias_ref, cot_ref,
    out_ref, gw_ref, gb_ref,
    rows_at, cols, counts, bias, gath, adj_in, adj_hi, adj_lo, prod, m_out, c1_in, s_buf,
    relay, direct, mid, final, away, mt, w_full, cot, out_v,
    g_buf, f1_in, f2_in, f3_in, p2, p3, b_one, b_two, b1_in, b2_in,
    zr, xr, xo, zs, xs, lsem, asem, wsem, csem, ysem, ysend, dsem, fsem,
):
    row, col, rep = lax.axis_index("row"), lax.axis_index("col"), lax.axis_index("rep")
    x_lo, z = row // nz, row % nz
    y, core = col // 2, col % 2
    far = nz // 2
    width, block = feat_ref.shape
    half_w, half_b = width // 2, block // 2

    z_dev = ({"row": x_lo * nz + (z + 1) % nz}, {"row": x_lo * nz + (z + nz - 1) % nz})
    x_dev = {"row": (1 - x_lo) * nz + z}
    core_dev = {"col": y * 2 + 1 - core}
    y_dev = ({"col": ((y + 1) % NY) * 2 + core}, {"col": ((y + NY - 1) % NY) * 2 + core})
    rep_dev = {"rep": 1 - rep}

    barrier = pltpu.get_barrier_semaphore()
    for device in (*z_dev, x_dev, core_dev, *y_dev, rep_dev):
        pl.semaphore_signal(barrier, inc=1, device_id=device, device_id_type=MESH)

    adj_copies = [pltpu.make_async_copy(adj_ref.at[0, 0, t], adj_in.at[t], asem.at[t]) for t in range(4)]
    own_copy = pltpu.make_async_copy(feat_ref, gath.at[row], lsem.at[0])
    cot_copy = pltpu.make_async_copy(cot_ref, cot, lsem.at[1])
    w_copy = pltpu.make_async_copy(weight_ref, w_full.at[pl.ds(rep * width, width)], lsem.at[2])
    bias_copy = pltpu.make_async_copy(bias_ref, bias, lsem.at[4])
    ints = ((rows_ref, rows_at), (cols_ref, cols), (counts_ref, counts))
    int_copies = [pltpu.make_async_copy(source, place, lsem.at[5 + k]) for k, (source, place) in enumerate(ints)]

    pl.semaphore_wait(barrier, 7)

    def slot(plane, hops, way):
        return plane * nz + (z + nz - hops if way == 0 else z + hops) % nz

    def rows_of(way, c):
        return pl.ds((c if way == 0 else 3 - c) * CHUNK, CHUNK)

    def over_z(other, hops, way, c, first=False):
        plane = 1 - x_lo if other else x_lo
        place = slot(plane, hops - 1, way)
        source = feat_ref if first else gath.at[place]
        rows = rows_of(way, c)
        return remote(
            source.at[rows],
            gath.at[place, rows],
            zs.at[other],
            zr.at[way, hops - 1, c + 2 if other else c],
            z_dev[way],
        )

    def landed_z(other, hops, way, c):
        place = gath.at[slot(1 - x_lo if other else x_lo, hops, way), rows_of(way, c)]
        remote(place, place, zs.at[0], zr.at[way, hops - 1, c + 2 if other else c], z_dev[way]).wait_recv()

    def over_x(hops, way, c):
        piece = gath.at[slot(x_lo, hops, way), rows_of(way, c)]
        return remote(piece, piece, xs.at[0], xr.at[way, hops - 1, c], x_dev)

    def landed_x(hops, way, c):
        piece = gath.at[slot(1 - x_lo, hops, way), rows_of(way, c)]
        remote(piece, piece, xs.at[0], xr.at[way, hops - 1, c], x_dev).wait_recv()

    def own_over_x(c, place):
        rows = rows_of(0, c)
        return remote(feat_ref.at[rows], gath.at[place, rows], xs.at[0], xo.at[c], x_dev)

    def over_x_count(hops):
        return 3 if hops < far - 1 else 2

    for c in (3, 0):
        own_over_x(c, row).start()
    for c in OWN_ORDER:
        for way in (0, 1):
            over_z(0, 1, way, c, True).start()
    for c in (2, 1):
        own_over_x(c, row).start()
    own_copies = (own_copy, cot_copy, w_copy, bias_copy, *int_copies)
    for copy in (*adj_copies, *own_copies):
        copy.start()
    w_send = remote(weight_ref, w_full.at[pl.ds(rep * width, width)], wsem.at[0], wsem.at[1], rep_dev)
    w_send.start()

    step = 32
    steps = block // step * 4

    def split(first, count):
        def one(i, carry):
            t, low = i // (block // step), pl.multiple_of((i % (block // step)) * step, step)
            value = adj_in[t, pl.ds(low, step), :]
            high = value.astype(BF16)
            adj_hi[t, pl.ds(low, step), :] = high
            adj_lo[t, pl.ds(low, step), :] = (value - high.astype(F32)).astype(BF16)
            return carry

        lax.fori_loop(first, first + count, one, 0)

    partner = (1 - x_lo) * nz + z
    for way, c in ((0, 3), (1, 0)):
        own_over_x(c, partner).wait_recv()
        over_z(1, 1, way, 3).start()
    done = 0
    for hops in range(1, far):
        last = hops == far - 1
        for c in OWN_ORDER:
            for way in (0, 1):
                landed_z(0, hops, way, c)
                if not last or c >= 2:
                    over_z(0, hops + 1, way, c).start()
                if c < over_x_count(hops):
                    over_x(hops, way, c).start()
        if last:
            for way in (0, 1):
                landed_x(far - 2, way, 2)
                over_z(1, far - 1, way, 2).start()
        for way in (0, 1):
            landed_z(1, hops, way, 3)
            over_z(1, hops + 1, way, 3).start()
        if hops == 1:
            for copy in adj_copies:
                copy.wait()
        upto = steps * hops // (far - 1)
        split(done, upto - done)
        done = upto
    for way in (0, 1):
        landed_z(1, far - 1, way, 2)
        over_z(1, far, way, 2).start()
    for c in (1, 2):
        own_over_x(c, partner).wait_recv()
    for hops in range(1, far):
        for c in range(over_x_count(hops)):
            for way in (0, 1):
                if (hops, c) != (far - 2, 2):
                    landed_x(hops, way, c)
    for copy in own_copies:
        copy.wait()
    for c in (2, 3):
        for way in (0, 1):
            landed_z(0, far, way, c)
    for c in (3, 2):
        for way in (0, 1):
            landed_z(1, far, way, c)

    count = counts[0, 0]
    for t in range(4):
        value = gath[jnp.clip(cols[0, 0, t], 0, 2 * nz - 1)]
        high = value.astype(BF16)
        low = (value - high.astype(F32)).astype(BF16)
        dims = (((1,), (1,)), ((), ()))
        both = lax.dot_general(jnp.concatenate([high, low], axis=0), adj_hi[t], dims, preferred_element_type=F32)
        rest = lax.dot_general(high, adj_lo[t], dims, preferred_element_type=F32)
        product = both[:width] + both[width:] + rest
        for h in (0, 1):
            prod[t, h] = product[:, h * half_b : (h + 1) * half_b]

    def placed(group, h):
        total = None
        for t in range(4):
            scale = jnp.where((t < count) & (rows_at[0, 0, t] == group), F32(1.0), F32(0.0))
            term = prod[t, h] * scale
            total = term if total is None else total + term
        return total

    order = ((0, 1 - rep), (1, rep))
    core_copies = {}
    for n, h in order:
        for k, offset in enumerate(OFFSETS):
            m_out[n, k] = placed(((y + offset) % NY) * 2 + 1 - core, h)
            copy = remote(m_out.at[n, k], c1_in.at[n, k], csem.at[0, n, k], csem.at[1, n, k], core_dev)
            copy.start()
            core_copies[n, k] = copy
    up, down = pl.ds(0, half_w), pl.ds(half_w, half_w)
    y_copies = {}

    def over_y(src, dst, name, n, way):
        index = ("relay0", "relay1", "direct0", "direct1", "final0", "final1").index(name) * 2 + n
        copy = remote(src, dst, ysend.at[index], ysem.at[index], y_dev[way])
        copy.start()
        y_copies[name, n] = copy

    for n, h in order:
        for k, offset in enumerate(OFFSETS):
            total = placed(((y + offset) % NY) * 2 + core, h)
            core_copies[n, k].wait_recv()
            s_buf[n, k] = total + c1_in[n, k]
            if offset == 2:
                over_y(s_buf.at[n, k, up], relay.at[0, n], "relay0", n, 0)
                over_y(s_buf.at[n, k, down], relay.at[1, n], "relay1", n, 1)
            elif offset == 1:
                over_y(s_buf.at[n, k, down], direct.at[1, n], "direct1", n, 0)
            elif offset == 3:
                over_y(s_buf.at[n, k, up], direct.at[0, n], "direct0", n, 1)
    for n in (0, 1):
        y_copies["relay0", n].wait_recv()
        mid[0, n] = relay[0, n] + s_buf[n, 1, up]
        over_y(mid.at[0, n], final.at[0, n], "final0", n, 0)
        y_copies["relay1", n].wait_recv()
        mid[1, n] = relay[1, n] + s_buf[n, 2, down]
        over_y(mid.at[1, n], final.at[1, n], "final1", n, 1)
    away_copy = remote(away, mt.at[pl.ds(rep * width, width)], dsem.at[0], dsem.at[1], rep_dev)
    for n in (0, 1):
        for part in (0, 1):
            y_copies["direct%d" % part, n].wait_recv()
            y_copies["final%d" % part, n].wait_recv()
            rows = pl.ds(part * half_w, half_w)
            total = s_buf[n, 3, rows] + final[part, n] + direct[part, n]
            if n == 0:
                away[rows] = total
            else:
                mt[pl.ds(pl.multiple_of(rep * width + part * half_w, half_w), half_w), :] = total
        if n == 0:
            away_copy.start()
    w_send.wait_recv()
    away_copy.wait_recv()

    preact = jnp.dot(mt[...].T, w_full[...], precision=HIGHEST, preferred_element_type=F32) + bias[...]
    squash = 1.0 / (1.0 + jnp.exp(-preact))
    out_v[...] = preact * squash
    out_copy = pltpu.make_async_copy(out_v, out_ref, lsem.at[3])
    out_copy.start()
    slope = cot[...] * squash * (1.0 + preact * (1.0 - squash))
    grad = jnp.dot(mt[...], slope, precision=HIGHEST, preferred_element_type=F32)
    for k in range(PIECES):
        g_buf[k] = grad[4 * k : 4 * k + 4]
    b_one[...] = jnp.sum(slope, axis=0, keepdims=True)

    def in_plane(peer):
        return {"row": (peer // 8 % 2) * nz + z, "col": peer % 8, "rep": peer // 16}

    me = rep * 16 + x_lo * 8 + col
    for j in range(1, PIECES):
        peer = (me + j) % PIECES
        remote(g_buf.at[peer], f1_in.at[j - 1], fsem.at[0], fsem.at[1], in_plane(peer)).start()
        remote(b_one, b1_in.at[j - 1], fsem.at[2], fsem.at[3], in_plane(peer)).start()
    own_piece, own_bias = g_buf[me], b_one[...]
    remote(f1_in, f1_in, fsem.at[0], fsem.at[1], rep_dev).wait_recv()
    remote(b1_in, b1_in, fsem.at[2], fsem.at[3], rep_dev).wait_recv()
    mine = jnp.sum(f1_in[...], axis=0) + own_piece
    bias_sum = jnp.sum(b1_in[...], axis=0) + own_bias
    p2[...] = mine
    f2_in[z] = mine
    b_two[...] = bias_sum
    b2_in[z] = bias_sum
    for k in sorted(range(1, nz), key=lambda j: -min(j, nz - j)):
        device = {"row": x_lo * nz + (z + k) % nz}
        remote(p2, f2_in.at[z], fsem.at[4], fsem.at[5], device).start()
        remote(b_two, b2_in.at[z], fsem.at[6], fsem.at[7], device).start()
    others = pl.ds(0, nz - 1)
    remote(f2_in.at[others], f2_in.at[others], fsem.at[4], fsem.at[5], rep_dev).wait_recv()
    mine = jnp.sum(f2_in[...], axis=0)
    p3[...] = mine
    here = x_lo * 8 + col
    f3_in[here] = mine
    for j in range(1, 16):
        device = in_plane(rep * 16 + (here + j) % 16)
        remote(p3, f3_in.at[here], fsem.at[8], fsem.at[9], device).start()
    remote(b2_in.at[others], b2_in.at[others], fsem.at[6], fsem.at[7], rep_dev).wait()
    gb_ref[...] = jnp.sum(b2_in[...], axis=0)
    f3_others = f3_in.at[pl.ds(0, 15)]
    remote(f3_others, f3_others, fsem.at[8], fsem.at[9], rep_dev).wait()
    for k in range(16):
        gw_ref[4 * k : 4 * k + 4, :] = f3_in[k]

    out_copy.wait()
    part = gath.at[pl.ds(0, nz - 1)]
    remote(part, part, zs.at[0], xo.at[0], rep_dev).wait_send()
    part = gath.at[pl.ds(0, far // 2 + 1)]
    remote(part, part, zs.at[1], xo.at[0], rep_dev).wait_send()
    part = gath.at[pl.ds(0, 3 * (far - 2) // 2 + 2)]
    remote(part, part, xs.at[0], xo.at[0], rep_dev).wait_send()
    w_send.wait_send()
    away_copy.wait_send()
    for copy in (*core_copies.values(), *y_copies.values()):
        copy.wait_send()
    remote(f1_in, f1_in, fsem.at[0], fsem.at[1], rep_dev).wait_send()
    remote(b1_in, b1_in, fsem.at[2], fsem.at[3], rep_dev).wait_send()
    remote(f2_in.at[others], f2_in.at[others], fsem.at[4], fsem.at[5], rep_dev).wait_send()


def solution(mesh):
    nz = mesh.shape["row"] // 2

    def local(adj_tiles, tile_rows, tile_cols, tile_counts, features_t, weight, bias_vec, cotangent):
        width, block = features_t.shape
        half_w, half_b = width // 2, block // 2
        out_w = weight.shape[1]
        nodes = cotangent.shape[0]
        vmem = pl.BlockSpec(memory_space=pltpu.VMEM)
        hbm = pl.BlockSpec(memory_space=pltpu.HBM)
        dma = pltpu.SemaphoreType.DMA
        output, grad_weight, grad_bias = pl.pallas_call(
            functools.partial(kernel, nz),
            out_shape=(
                jax.ShapeDtypeStruct((nodes, out_w), F32),
                jax.ShapeDtypeStruct((width, out_w), F32),
                jax.ShapeDtypeStruct((1, out_w), F32),
            ),
            in_specs=[hbm] * 8,
            out_specs=(hbm, vmem, vmem),
            scratch_shapes=[
                pltpu.SMEM(tile_rows.shape, jnp.int32),
                pltpu.SMEM(tile_cols.shape, jnp.int32),
                pltpu.SMEM(tile_counts.shape, jnp.int32),
                pltpu.VMEM((1, out_w), F32),
                pltpu.VMEM((2 * nz, width, block), F32),
                pltpu.VMEM((4, block, block), F32),
                pltpu.VMEM((4, block, block), BF16),
                pltpu.VMEM((4, block, block), BF16),
                pltpu.VMEM((4, 2, width, half_b), F32),
                pltpu.VMEM((2, 4, width, half_b), F32),
                pltpu.VMEM((2, 4, width, half_b), F32),
                pltpu.VMEM((2, 4, width, half_b), F32),
                pltpu.VMEM((2, 2, half_w, half_b), F32),
                pltpu.VMEM((2, 2, half_w, half_b), F32),
                pltpu.VMEM((2, 2, half_w, half_b), F32),
                pltpu.VMEM((2, 2, half_w, half_b), F32),
                pltpu.VMEM((width, half_b), F32),
                pltpu.VMEM((2 * width, half_b), F32),
                pltpu.VMEM((2 * width, out_w), F32),
                pltpu.VMEM((nodes, out_w), F32),
                pltpu.VMEM((nodes, out_w), F32),
                pltpu.VMEM((PIECES, 4, out_w), F32),
                pltpu.VMEM((PIECES - 1, 4, out_w), F32),
                pltpu.VMEM((nz, 4, out_w), F32),
                pltpu.VMEM((16, 4, out_w), F32),
                pltpu.VMEM((4, out_w), F32),
                pltpu.VMEM((4, out_w), F32),
                pltpu.VMEM((1, out_w), F32),
                pltpu.VMEM((1, out_w), F32),
                pltpu.VMEM((PIECES - 1, 1, out_w), F32),
                pltpu.VMEM((nz, 1, out_w), F32),
                dma((2, nz // 2, 6)),
                dma((2, nz // 2 - 1, 3)),
                dma((4,)),
                dma((2,)),
                dma((1,)),
                dma((8,)),
                dma((4,)),
                dma((2,)),
                dma((2, 2, 4)),
                dma((12,)),
                dma((12,)),
                dma((2,)),
                dma((12,)),
            ],
            compiler_params=pltpu.CompilerParams(
                collective_id=0, has_side_effects=True, vmem_limit_bytes=67043328
            ),
        )(tile_rows, tile_cols, tile_counts, adj_tiles, features_t, weight, bias_vec.reshape(1, out_w), cotangent)
        return output, grad_weight, grad_bias.reshape(out_w)

    return jax.shard_map(
        local,
        mesh=mesh,
        in_specs=(
            P("row", "col", None, None, None),
            P("row", "col", None),
            P("row", "col", None),
            P("row", "col"),
            P("rep", ("row", "col")),
            P("rep", None),
            P(),
            P(("row", "col", "rep"), None),
        ),
        out_specs=(P(("row", "col", "rep"), None), P("rep", None), P()),
        check_vma=False,
    )
```

time: 93.2 us -> 86.8 us (0.931)
  local copies, waits for them, and re-layouts: 8.49 us -> 4.08 us
  Pallas kernels: 83.1 us -> 81.2 us
    unnamed x17 -> x3, local copies, waits for them, and re-layouts: 8.49 us -> 4.08 us
    pallas_call x1, Pallas kernels: 83.1 us -> 81.2 us  [local(): pl.pallas_call(functools.partial(kernel, nz), out_shape=(jax.ShapeDtypeSt...]
where the time goes in v2:
time: 86.8 us; the launch traced here: 86.6 us
  Pallas kernels  81.2 us (94%)
  local copies, waits for them, and re-layouts  4.08 us (5%)
  between operations  1.29 us (1%)
    pallas_call x1, Pallas kernels, local(): pl.pallas_call(functools.partial(kernel, nz), out_shape=(jax.ShapeDtypeSt...  81.2 us
    unnamed x3, local copies, waits for them, and re-layouts  4.08 us

profile of v2, /device:TPU:1, one launch (start us, length us, event | category | flops | bytes accessed | tf_op | source)
XLA Modules:
  0.0 86.6 jit_solution(9967551552433277339)
XLA Ops:
  1.3 81.2 %shard_map.103 = (f32[256,128]{1,0:T(8,128)}, f32[64,128]{1,0:T(8,128)}, f32[1,128]{1,0:T(1,128)}) custom-call(s32[1,1,4]{2,1,0:T(1,128)} %rows_ref.1, s32[1,1,4]{2,1,0:T(1,128)} %cols_ref.1, s32[1,1]{1,0:T(1,128)S(6)} %copy.14.counts_ref, f32[1,1,4,512,512]{4,3,2,1,0:T(8,128)} %adj_ref.1, f32[64,512]{1,0:T(8,128)} %feat_ref.1, f32[64,128]{1,0:T(8,128)} %weight_ref.1, ...), custom_call_target="tpu_custom_call" | custom-call | tf_op jit(solution)/shard_map/pallas_call | solution.py:322
  82.5 1.6 %copy.15 = f32[256,128]{1,0:T(8,128)} copy(f32[256,128]{1,0:T(8,128)} %get-tuple-element.12) | data formatting | bytes 262144
  84.1 1.4 %copy.16 = f32[64,128]{1,0:T(8,128)} copy(f32[64,128]{1,0:T(8,128)} %get-tuple-element.13) | data formatting | bytes 65536
  85.5 1.1 %copy.17 = f32[128]{0:T(128)} copy(f32[128]{0:T(128)} %bitcast.3) | data formatting | bytes 1024

commit v3 on v2

--- a/solution.py
+++ b/solution.py
@@ -16,7 +16,7 @@
 PIECES = 32
 CHUNK = 16
 OWN_ORDER = (2, 0, 1, 3)
-OFFSETS = (2, 1, 3, 0)
+SENDING = ((0, 2), (0, 1), (0, 3), (1, 2), (0, 0), (1, 1), (1, 3), (1, 0))
 
 
 def remote(src, dst, send_sem, recv_sem, device):
@@ -30,9 +30,9 @@
     rows_ref, cols_ref, counts_ref, adj_ref, feat_ref, weight_ref, bias_ref, cot_ref,
     out_ref, gw_ref, gb_ref,
     rows_at, cols, counts, bias, gath, adj_in, adj_hi, adj_lo, prod, m_out, c1_in, s_buf,
-    relay, direct, mid, final, away, mt, w_full, cot, out_v,
-    g_buf, f1_in, f2_in, f3_in, p2, p3, b_one, b_two, b1_in, b2_in,
-    zr, xr, xo, zs, xs, lsem, asem, wsem, csem, ysem, ysend, dsem, fsem,
+    y_in, mt, w_full, cot, out_v,
+    g_buf, f1_in, f2_in, f3_in, p2, p3,
+    zr, xr, xo, zs, xs, lsem, asem, wsem, csem, ysem, fsem, ready,
 ):
     row, col, rep = lax.axis_index("row"), lax.axis_index("col"), lax.axis_index("rep")
     x_lo, z = row // nz, row % nz
@@ -47,6 +47,13 @@
     y_dev = ({"col": ((y + 1) % NY) * 2 + core}, {"col": ((y + NY - 1) % NY) * 2 + core})
     rep_dev = {"rep": 1 - rep}
 
+    cols_of = [col] + [(col + j) % 8 for j in range(1, 8)]
+    planes = []
+    for i in range(4):
+        x = (rep * 2 + x_lo + i) % 4
+        planes.append((x // 2 * 16 + x % 2 * 8, x % 2 * nz + z, x // 2))
+    z_devs = [{"row": x_lo * nz + (z + k) % nz} for k in sorted(range(1, nz), key=lambda j: -min(j, nz - j))]
+
     barrier = pltpu.get_barrier_semaphore()
     for device in (*z_dev, x_dev, core_dev, *y_dev, rep_dev):
         pl.semaphore_signal(barrier, inc=1, device_id=device, device_id_type=MESH)
@@ -60,6 +67,9 @@
     int_copies = [pltpu.make_async_copy(source, place, lsem.at[5 + k]) for k, (source, place) in enumerate(ints)]
 
     pl.semaphore_wait(barrier, 7)
+    near = (*y_dev, rep_dev)
+    for device in near:
+        pl.semaphore_signal(ready.at[0], inc=1, device_id=device, device_id_type=MESH)
 
     def slot(plane, hops, way):
         return plane * nz + (z + nz - hops if way == 0 else z + hops) % nz
@@ -150,6 +160,10 @@
         if hops == 1:
             for copy in adj_copies:
                 copy.wait()
+        if hops == 3:
+            pl.semaphore_wait(ready.at[0], 3)
+            for device in near:
+                pl.semaphore_signal(ready.at[1], inc=1, device_id=device, device_id_type=MESH)
         upto = steps * hops // (far - 1)
         split(done, upto - done)
         done = upto
@@ -165,6 +179,7 @@
                     landed_x(hops, way, c)
     for copy in own_copies:
         copy.wait()
+    pl.semaphore_wait(ready.at[1], 3)
     for c in (2, 3):
         for way in (0, 1):
             landed_z(0, far, way, c)
@@ -194,55 +209,27 @@
 
     order = ((0, 1 - rep), (1, rep))
     core_copies = {}
-    for n, h in order:
-        for k, offset in enumerate(OFFSETS):
-            m_out[n, k] = placed(((y + offset) % NY) * 2 + 1 - core, h)
-            copy = remote(m_out.at[n, k], c1_in.at[n, k], csem.at[0, n, k], csem.at[1, n, k], core_dev)
+    for n, k in SENDING:
+        m_out[n, k] = placed(((y + k) % NY) * 2 + 1 - core, order[n][1])
+        copy = remote(m_out.at[n, k], c1_in.at[n, k], csem.at[0, n, k], csem.at[1, n, k], core_dev)
+        copy.start()
+        core_copies[n, k] = copy
+    y_copies = {}
+    for n, k in SENDING:
+        total = placed(((y + k) % NY) * 2 + core, order[n][1])
+        core_copies[n, k].wait_recv()
+        s_buf[n, k] = total + c1_in[n, k]
+        if (n, k) != (1, 0):
+            device = {"col": ((y + k) % NY) * 2 + core, "rep": order[n][1]}
+            copy = remote(s_buf.at[n, k], y_in.at[n, k], ysem.at[0, n, k], ysem.at[1, n, k], device)
             copy.start()
-            core_copies[n, k] = copy
-    up, down = pl.ds(0, half_w), pl.ds(half_w, half_w)
-    y_copies = {}
-
-    def over_y(src, dst, name, n, way):
-        index = ("relay0", "relay1", "direct0", "direct1", "final0", "final1").index(name) * 2 + n
-        copy = remote(src, dst, ysend.at[index], ysem.at[index], y_dev[way])
-        copy.start()
-        y_copies[name, n] = copy
-
-    for n, h in order:
-        for k, offset in enumerate(OFFSETS):
-            total = placed(((y + offset) % NY) * 2 + core, h)
-            core_copies[n, k].wait_recv()
-            s_buf[n, k] = total + c1_in[n, k]
-            if offset == 2:
-                over_y(s_buf.at[n, k, up], relay.at[0, n], "relay0", n, 0)
-                over_y(s_buf.at[n, k, down], relay.at[1, n], "relay1", n, 1)
-            elif offset == 1:
-                over_y(s_buf.at[n, k, down], direct.at[1, n], "direct1", n, 0)
-            elif offset == 3:
-                over_y(s_buf.at[n, k, up], direct.at[0, n], "direct0", n, 1)
-    for n in (0, 1):
-        y_copies["relay0", n].wait_recv()
-        mid[0, n] = relay[0, n] + s_buf[n, 1, up]
-        over_y(mid.at[0, n], final.at[0, n], "final0", n, 0)
-        y_copies["relay1", n].wait_recv()
-        mid[1, n] = relay[1, n] + s_buf[n, 2, down]
-        over_y(mid.at[1, n], final.at[1, n], "final1", n, 1)
-    away_copy = remote(away, mt.at[pl.ds(rep * width, width)], dsem.at[0], dsem.at[1], rep_dev)
-    for n in (0, 1):
-        for part in (0, 1):
-            y_copies["direct%d" % part, n].wait_recv()
-            y_copies["final%d" % part, n].wait_recv()
-            rows = pl.ds(part * half_w, half_w)
-            total = s_buf[n, 3, rows] + final[part, n] + direct[part, n]
-            if n == 0:
-                away[rows] = total
-            else:
-                mt[pl.ds(pl.multiple_of(rep * width + part * half_w, half_w), half_w), :] = total
-        if n == 0:
-            away_copy.start()
+            y_copies[n, k] = copy
+    for n, k in SENDING:
+        if (n, k) in y_copies:
+            y_copies[n, k].wait_recv()
+    mt[pl.ds(pl.multiple_of(rep * width, width), width), :] = s_buf[1, 0] + y_in[1, 1] + y_in[1, 2] + y_in[1, 3]
+    mt[pl.ds(pl.multiple_of((1 - rep) * width, width), width), :] = y_in[0, 0] + y_in[0, 1] + y_in[0, 2] + y_in[0, 3]
     w_send.wait_recv()
-    away_copy.wait_recv()
 
     preact = jnp.dot(mt[...].T, w_full[...], precision=HIGHEST, preferred_element_type=F32) + bias[...]
     squash = 1.0 / (1.0 + jnp.exp(-preact))
@@ -251,44 +238,38 @@
     out_copy.start()
     slope = cot[...] * squash * (1.0 + preact * (1.0 - squash))
     grad = jnp.dot(mt[...], slope, precision=HIGHEST, preferred_element_type=F32)
+    bias_row = jnp.sum(slope, axis=0, keepdims=True)
     for k in range(PIECES):
-        g_buf[k] = grad[4 * k : 4 * k + 4]
-    b_one[...] = jnp.sum(slope, axis=0, keepdims=True)
-
-    def in_plane(peer):
-        return {"row": (peer // 8 % 2) * nz + z, "col": peer % 8, "rep": peer // 16}
-
-    me = rep * 16 + x_lo * 8 + col
-    for j in range(1, PIECES):
-        peer = (me + j) % PIECES
-        remote(g_buf.at[peer], f1_in.at[j - 1], fsem.at[0], fsem.at[1], in_plane(peer)).start()
-        remote(b_one, b1_in.at[j - 1], fsem.at[2], fsem.at[3], in_plane(peer)).start()
-    own_piece, own_bias = g_buf[me], b_one[...]
+        g_buf[k, 0:4] = grad[4 * k : 4 * k + 4]
+        g_buf[k, 4:5] = bias_row
+
+    for i in range(4):
+        for j in range(8):
+            if i + j > 0:
+                piece, slot_at = planes[i][0] + cols_of[j], i * 8 + j - 1
+                device = {"row": planes[i][1], "rep": planes[i][2], "col": cols_of[j]}
+                remote(g_buf.at[piece], f1_in.at[slot_at], fsem.at[0], fsem.at[1], device).start()
+    own_piece = g_buf[planes[0][0] + col]
     remote(f1_in, f1_in, fsem.at[0], fsem.at[1], rep_dev).wait_recv()
-    remote(b1_in, b1_in, fsem.at[2], fsem.at[3], rep_dev).wait_recv()
     mine = jnp.sum(f1_in[...], axis=0) + own_piece
-    bias_sum = jnp.sum(b1_in[...], axis=0) + own_bias
     p2[...] = mine
     f2_in[z] = mine
-    b_two[...] = bias_sum
-    b2_in[z] = bias_sum
-    for k in sorted(range(1, nz), key=lambda j: -min(j, nz - j)):
-        device = {"row": x_lo * nz + (z + k) % nz}
-        remote(p2, f2_in.at[z], fsem.at[4], fsem.at[5], device).start()
-        remote(b_two, b2_in.at[z], fsem.at[6], fsem.at[7], device).start()
-    others = pl.ds(0, nz - 1)
-    remote(f2_in.at[others], f2_in.at[others], fsem.at[4], fsem.at[5], rep_dev).wait_recv()
+    for device in z_devs:
+        remote(p2, f2_in.at[z], fsem.at[2], fsem.at[3], device).start()
+    others = f2_in.at[pl.ds(0, nz - 1)]
+    remote(others, others, fsem.at[2], fsem.at[3], rep_dev).wait_recv()
     mine = jnp.sum(f2_in[...], axis=0)
-    p3[...] = mine
+    p3[...] = mine[0:4]
     here = x_lo * 8 + col
-    f3_in[here] = mine
-    for j in range(1, 16):
-        device = in_plane(rep * 16 + (here + j) % 16)
-        remote(p3, f3_in.at[here], fsem.at[8], fsem.at[9], device).start()
-    remote(b2_in.at[others], b2_in.at[others], fsem.at[6], fsem.at[7], rep_dev).wait()
-    gb_ref[...] = jnp.sum(b2_in[...], axis=0)
+    f3_in[here] = mine[0:4]
+    for i in (0, 1):
+        for j in range(8):
+            if i + j > 0:
+                device = {"row": (x_lo + i - 2 * i * x_lo) * nz + z, "col": cols_of[j]}
+                remote(p3, f3_in.at[here], fsem.at[4], fsem.at[5], device).start()
+    gb_ref[...] = mine[4:5]
     f3_others = f3_in.at[pl.ds(0, 15)]
-    remote(f3_others, f3_others, fsem.at[8], fsem.at[9], rep_dev).wait()
+    remote(f3_others, f3_others, fsem.at[4], fsem.at[5], rep_dev).wait()
     for k in range(16):
         gw_ref[4 * k : 4 * k + 4, :] = f3_in[k]
 
@@ -300,12 +281,16 @@
     part = gath.at[pl.ds(0, 3 * (far - 2) // 2 + 2)]
     remote(part, part, xs.at[0], xo.at[0], rep_dev).wait_send()
     w_send.wait_send()
-    away_copy.wait_send()
     for copy in (*core_copies.values(), *y_copies.values()):
         copy.wait_send()
     remote(f1_in, f1_in, fsem.at[0], fsem.at[1], rep_dev).wait_send()
-    remote(b1_in, b1_in, fsem.at[2], fsem.at[3], rep_dev).wait_send()
-    remote(f2_in.at[others], f2_in.at[others], fsem.at[4], fsem.at[5], rep_dev).wait_send()
+    remote(others, others, fsem.at[2], fsem.at[3], rep_dev).wait_send()
+
+
+def hand_over(output, grad_weight, grad_bias, out_ref, gw_ref, gb_ref):
+    out_ref[...] = output[...]
+    gw_ref[...] = grad_weight[...]
+    gb_ref[...] = grad_bias[...]
 
 
 def solution(mesh):
@@ -341,25 +326,17 @@
                 pltpu.VMEM((2, 4, width, half_b), F32),
                 pltpu.VMEM((2, 4, width, half_b), F32),
                 pltpu.VMEM((2, 4, width, half_b), F32),
-                pltpu.VMEM((2, 2, half_w, half_b), F32),
-                pltpu.VMEM((2, 2, half_w, half_b), F32),
-                pltpu.VMEM((2, 2, half_w, half_b), F32),
-                pltpu.VMEM((2, 2, half_w, half_b), F32),
-                pltpu.VMEM((width, half_b), F32),
+                pltpu.VMEM((2, 4, width, half_b), F32),
                 pltpu.VMEM((2 * width, half_b), F32),
                 pltpu.VMEM((2 * width, out_w), F32),
                 pltpu.VMEM((nodes, out_w), F32),
                 pltpu.VMEM((nodes, out_w), F32),
-                pltpu.VMEM((PIECES, 4, out_w), F32),
-                pltpu.VMEM((PIECES - 1, 4, out_w), F32),
-                pltpu.VMEM((nz, 4, out_w), F32),
+                pltpu.VMEM((PIECES, 5, out_w), F32),
+                pltpu.VMEM((PIECES - 1, 5, out_w), F32),
+                pltpu.VMEM((nz, 5, out_w), F32),
                 pltpu.VMEM((16, 4, out_w), F32),
+                pltpu.VMEM((5, out_w), F32),
                 pltpu.VMEM((4, out_w), F32),
-                pltpu.VMEM((4, out_w), F32),
-                pltpu.VMEM((1, out_w), F32),
-                pltpu.VMEM((1, out_w), F32),
-                pltpu.VMEM((PIECES - 1, 1, out_w), F32),
-                pltpu.VMEM((nz, 1, out_w), F32),
                 dma((2, nz // 2, 6)),
                 dma((2, nz // 2 - 1, 3)),
                 dma((4,)),
@@ -369,15 +346,20 @@
                 dma((4,)),
                 dma((2,)),
                 dma((2, 2, 4)),
-                dma((12,)),
-                dma((12,)),
-                dma((2,)),
-                dma((12,)),
+                dma((2, 2, 4)),
+                dma((6,)),
+                pltpu.SemaphoreType.REGULAR((2,)),
             ],
             compiler_params=pltpu.CompilerParams(
                 collective_id=0, has_side_effects=True, vmem_limit_bytes=67043328
             ),
         )(tile_rows, tile_cols, tile_counts, adj_tiles, features_t, weight, bias_vec.reshape(1, out_w), cotangent)
+        output, grad_weight, grad_bias = pl.pallas_call(
+            hand_over,
+            out_shape=tuple(jax.ShapeDtypeStruct(a.shape, F32) for a in (output, grad_weight, grad_bias)),
+            in_specs=[vmem] * 3,
+            out_specs=(vmem,) * 3,
+        )(output, grad_weight, grad_bias)
         return output, grad_weight, grad_bias.reshape(out_w)
 
     return jax.shard_map(

time: 86.8 us -> 81.6 us (0.940)
  local copies, waits for them, and re-layouts: 4.08 us -> 0 us
  Pallas kernels: 81.2 us -> 80.2 us
    unnamed x3 -> x0, local copies, waits for them, and re-layouts: 4.08 us -> none
    pallas_call x1, Pallas kernels: 81.2 us -> 78.6 us  [local(): pl.pallas_call(functools.partial(kernel, nz), out_shape=(jax.ShapeDtypeSt...]
    pallas_call x0 -> x1, Pallas kernels: none -> 1.6 us  [local(): pl.pallas_call(hand_over, out_shape=tuple((jax.ShapeDtypeStruct(a.shape,...]
where the time goes in v3:
time: 81.6 us; the launch traced here: 81.4 us
  Pallas kernels  80.2 us (98%)
  between operations  1.29 us (2%)
    pallas_call x1, Pallas kernels, local(): pl.pallas_call(functools.partial(kernel, nz), out_shape=(jax.ShapeDtypeSt...  78.6 us

profile of v3, /device:TPU:1, one launch (start us, length us, event | category | flops | bytes accessed | tf_op | source)
XLA Modules:
  0.0 81.4 jit_solution(1842996011938799515)
XLA Ops:
  1.3 78.6 %shard_map.103 = (f32[256,128]{1,0:T(8,128)}, f32[64,128]{1,0:T(8,128)}, f32[1,128]{1,0:T(1,128)}) custom-call(s32[1,1,4]{2,1,0:T(1,128)} %rows_ref.1, s32[1,1,4]{2,1,0:T(1,128)} %cols_ref.1, s32[1,1]{1,0:T(1,128)S(6)} %copy.11.counts_ref, f32[1,1,4,512,512]{4,3,2,1,0:T(8,128)} %adj_ref.1, f32[64,512]{1,0:T(8,128)} %feat_ref.1, f32[64,128]{1,0:T(8,128)} %weight_ref.1, ...), custom_call_target="tpu_custom_call" | custom-call | tf_op jit(solution)/shard_map/pallas_call | solution.py:307
  79.8 1.6 %shard_map.104 = (f32[256,128]{1,0:T(8,128)}, f32[64,128]{1,0:T(8,128)}, f32[1,128]{1,0:T(1,128)}) custom-call(f32[256,128]{1,0:T(8,128)} %get-tuple-element.9.output, f32[64,128]{1,0:T(8,128)} %get-tuple-element.10.grad_weight, f32[1,128]{1,0:T(1,128)} %get-tuple-element.11.grad_bias), custom_call_target="tpu_custom_call" | custom-call | tf_op jit(solution)/shard_map/pallas_call | solution.py:357

commit v4 on v3

--- a/solution.py
+++ b/solution.py
@@ -10,19 +10,24 @@
 MESH = pl.DeviceIdType.MESH
 F32 = jnp.float32
 BF16 = jnp.bfloat16
-HIGHEST = lax.Precision.HIGHEST
 
 NY = 4
 PIECES = 32
 CHUNK = 16
 OWN_ORDER = (2, 0, 1, 3)
-SENDING = ((0, 2), (0, 1), (0, 3), (1, 2), (0, 0), (1, 1), (1, 3), (1, 0))
+X_COUNT = (3, 3, 3, 3, 3, 2, 2)
+SENDING = ((0, 2), (0, 1), (0, 3), (0, 0), (1, 2), (1, 1), (1, 3), (1, 0))
 
 
 def remote(src, dst, send_sem, recv_sem, device):
     return pltpu.make_async_remote_copy(
         src_ref=src, dst_ref=dst, send_sem=send_sem, recv_sem=recv_sem, device_id=device, device_id_type=MESH
     )
+
+
+def halves(value):
+    high = value.astype(BF16)
+    return high, (value - high.astype(F32)).astype(BF16)
 
 
 def kernel(
@@ -30,7 +35,7 @@
     rows_ref, cols_ref, counts_ref, adj_ref, feat_ref, weight_ref, bias_ref, cot_ref,
     out_ref, gw_ref, gb_ref,
     rows_at, cols, counts, bias, gath, adj_in, adj_hi, adj_lo, prod, m_out, c1_in, s_buf,
-    y_in, mt, w_full, cot, out_v,
+    y_in, mt, w_full, w_three, x_both, cot, out_v,
     g_buf, f1_in, f2_in, f3_in, p2, p3,
     zr, xr, xo, zs, xs, lsem, asem, wsem, csem, ysem, fsem, ready,
 ):
@@ -39,7 +44,7 @@
     y, core = col // 2, col % 2
     far = nz // 2
     width, block = feat_ref.shape
-    half_w, half_b = width // 2, block // 2
+    half_b = block // 2
 
     z_dev = ({"row": x_lo * nz + (z + 1) % nz}, {"row": x_lo * nz + (z + nz - 1) % nz})
     x_dev = {"row": (1 - x_lo) * nz + z}
@@ -106,9 +111,6 @@
         rows = rows_of(0, c)
         return remote(feat_ref.at[rows], gath.at[place, rows], xs.at[0], xo.at[c], x_dev)
 
-    def over_x_count(hops):
-        return 3 if hops < far - 1 else 2
-
     for c in (3, 0):
         own_over_x(c, row).start()
     for c in OWN_ORDER:
@@ -116,8 +118,8 @@
             over_z(0, 1, way, c, True).start()
     for c in (2, 1):
         own_over_x(c, row).start()
-    own_copies = (own_copy, cot_copy, w_copy, bias_copy, *int_copies)
-    for copy in (*adj_copies, *own_copies):
+    own_copies = (own_copy, cot_copy, bias_copy, *int_copies)
+    for copy in (*adj_copies, w_copy, *own_copies):
         copy.start()
     w_send = remote(weight_ref, w_full.at[pl.ds(rep * width, width)], wsem.at[0], wsem.at[1], rep_dev)
     w_send.start()
@@ -142,21 +144,25 @@
         over_z(1, 1, way, 3).start()
     done = 0
     for hops in range(1, far):
-        last = hops == far - 1
         for c in OWN_ORDER:
             for way in (0, 1):
                 landed_z(0, hops, way, c)
-                if not last or c >= 2:
+                if hops < far - 1 or c >= 2:
                     over_z(0, hops + 1, way, c).start()
-                if c < over_x_count(hops):
+                if c < X_COUNT[hops - 1]:
                     over_x(hops, way, c).start()
-        if last:
+        if hops > 1:
+            for c in range(X_COUNT[hops - 1], X_COUNT[hops - 2]):
+                for way in (0, 1):
+                    landed_x(hops - 1, way, c)
+                    over_z(1, hops, way, c).start()
+        following = X_COUNT[hops] if hops < far - 1 else 2
+        for c in (3, 2):
             for way in (0, 1):
-                landed_x(far - 2, way, 2)
-                over_z(1, far - 1, way, 2).start()
-        for way in (0, 1):
-            landed_z(1, hops, way, 3)
-            over_z(1, hops + 1, way, 3).start()
+                if c >= X_COUNT[hops - 1]:
+                    landed_z(1, hops, way, c)
+                    if c >= following:
+                        over_z(1, hops + 1, way, c).start()
         if hops == 1:
             for copy in adj_copies:
                 copy.wait()
@@ -164,18 +170,20 @@
             pl.semaphore_wait(ready.at[0], 3)
             for device in near:
                 pl.semaphore_signal(ready.at[1], inc=1, device_id=device, device_id_type=MESH)
+        if hops == 5:
+            w_send.wait_recv()
+            w_copy.wait()
+            w_high, w_low = halves(w_full[...])
+            w_three[...] = jnp.concatenate([w_high, w_low, w_high], axis=0)
         upto = steps * hops // (far - 1)
         split(done, upto - done)
         done = upto
-    for way in (0, 1):
-        landed_z(1, far - 1, way, 2)
-        over_z(1, far, way, 2).start()
     for c in (1, 2):
         own_over_x(c, partner).wait_recv()
     for hops in range(1, far):
-        for c in range(over_x_count(hops)):
+        for c in range(X_COUNT[hops - 1]):
             for way in (0, 1):
-                if (hops, c) != (far - 2, 2):
+                if hops == far - 1 or c < X_COUNT[hops]:
                     landed_x(hops, way, c)
     for copy in own_copies:
         copy.wait()
@@ -188,35 +196,36 @@
             landed_z(1, far, way, c)
 
     count = counts[0, 0]
+    order = ((0, 1 - rep), (1, rep))
     for t in range(4):
-        value = gath[jnp.clip(cols[0, 0, t], 0, 2 * nz - 1)]
-        high = value.astype(BF16)
-        low = (value - high.astype(F32)).astype(BF16)
-        dims = (((1,), (1,)), ((), ()))
-        both = lax.dot_general(jnp.concatenate([high, low], axis=0), adj_hi[t], dims, preferred_element_type=F32)
-        rest = lax.dot_general(high, adj_lo[t], dims, preferred_element_type=F32)
-        product = both[:width] + both[width:] + rest
-        for h in (0, 1):
-            prod[t, h] = product[:, h * half_b : (h + 1) * half_b]
-
-    def placed(group, h):
+        high, low = halves(gath[jnp.clip(cols[0, 0, t], 0, 2 * nz - 1)])
+        x_both[t] = jnp.concatenate([high, low], axis=0)
+
+    def placed(group, n):
         total = None
         for t in range(4):
             scale = jnp.where((t < count) & (rows_at[0, 0, t] == group), F32(1.0), F32(0.0))
-            term = prod[t, h] * scale
+            term = prod[n, t] * scale
             total = term if total is None else total + term
         return total
 
-    order = ((0, 1 - rep), (1, rep))
     core_copies = {}
-    for n, k in SENDING:
-        m_out[n, k] = placed(((y + k) % NY) * 2 + 1 - core, order[n][1])
-        copy = remote(m_out.at[n, k], c1_in.at[n, k], csem.at[0, n, k], csem.at[1, n, k], core_dev)
-        copy.start()
-        core_copies[n, k] = copy
+    for n, h in order:
+        for t in range(4):
+            nodes = pl.ds(pl.multiple_of(h * half_b, half_b), half_b)
+            dims = (((1,), (1,)), ((), ()))
+            both = lax.dot_general(x_both[t], adj_hi[t, nodes, :], dims, preferred_element_type=F32)
+            rest = lax.dot_general(x_both[t, 0:width], adj_lo[t, nodes, :], dims, preferred_element_type=F32)
+            prod[n, t] = both[:width] + both[width:] + rest
+        for k in (2, 1, 3, 0):
+            m_out[n, k] = placed(((y + k) % NY) * 2 + 1 - core, n)
+            copy = remote(m_out.at[n, k], c1_in.at[n, k], csem.at[0, n, k], csem.at[1, n, k], core_dev)
+            copy.start()
+            core_copies[n, k] = copy
+
     y_copies = {}
     for n, k in SENDING:
-        total = placed(((y + k) % NY) * 2 + core, order[n][1])
+        total = placed(((y + k) % NY) * 2 + core, n)
         core_copies[n, k].wait_recv()
         s_buf[n, k] = total + c1_in[n, k]
         if (n, k) != (1, 0):
@@ -229,22 +238,28 @@
             y_copies[n, k].wait_recv()
     mt[pl.ds(pl.multiple_of(rep * width, width), width), :] = s_buf[1, 0] + y_in[1, 1] + y_in[1, 2] + y_in[1, 3]
     mt[pl.ds(pl.multiple_of((1 - rep) * width, width), width), :] = y_in[0, 0] + y_in[0, 1] + y_in[0, 2] + y_in[0, 3]
-    w_send.wait_recv()
-
-    preact = jnp.dot(mt[...].T, w_full[...], precision=HIGHEST, preferred_element_type=F32) + bias[...]
+    mixed = mt[...]
+    high, low = halves(mixed.T)
+    preact = jnp.dot(jnp.concatenate([high, high, low], axis=1), w_three[...], preferred_element_type=F32) + bias[...]
     squash = 1.0 / (1.0 + jnp.exp(-preact))
     out_v[...] = preact * squash
     out_copy = pltpu.make_async_copy(out_v, out_ref, lsem.at[3])
     out_copy.start()
     slope = cot[...] * squash * (1.0 + preact * (1.0 - squash))
-    grad = jnp.dot(mt[...], slope, precision=HIGHEST, preferred_element_type=F32)
+    high, low = halves(mixed)
+    s_high, s_low = halves(slope)
+    grad = jnp.dot(
+        jnp.concatenate([high, high, low], axis=1),
+        jnp.concatenate([s_high, s_low, s_high], axis=0),
+        preferred_element_type=F32,
+    )
     bias_row = jnp.sum(slope, axis=0, keepdims=True)
     for k in range(PIECES):
         g_buf[k, 0:4] = grad[4 * k : 4 * k + 4]
         g_buf[k, 4:5] = bias_row
 
-    for i in range(4):
-        for j in range(8):
+    for i in (2, 1, 3, 0):
+        for j in (4, 3, 5, 2, 6, 1, 7, 0):
             if i + j > 0:
                 piece, slot_at = planes[i][0] + cols_of[j], i * 8 + j - 1
                 device = {"row": planes[i][1], "rep": planes[i][2], "col": cols_of[j]}
@@ -262,8 +277,8 @@
     p3[...] = mine[0:4]
     here = x_lo * 8 + col
     f3_in[here] = mine[0:4]
-    for i in (0, 1):
-        for j in range(8):
+    for i in (1, 0):
+        for j in (4, 3, 5, 2, 6, 1, 7, 0):
             if i + j > 0:
                 device = {"row": (x_lo + i - 2 * i * x_lo) * nz + z, "col": cols_of[j]}
                 remote(p3, f3_in.at[here], fsem.at[4], fsem.at[5], device).start()
@@ -276,9 +291,9 @@
     out_copy.wait()
     part = gath.at[pl.ds(0, nz - 1)]
     remote(part, part, zs.at[0], xo.at[0], rep_dev).wait_send()
-    part = gath.at[pl.ds(0, far // 2 + 1)]
+    part = gath.at[pl.ds(0, sum(4 - c for c in X_COUNT) + 2), pl.ds(0, 2 * CHUNK)]
     remote(part, part, zs.at[1], xo.at[0], rep_dev).wait_send()
-    part = gath.at[pl.ds(0, 3 * (far - 2) // 2 + 2)]
+    part = gath.at[pl.ds(0, sum(X_COUNT) + 2), pl.ds(0, 2 * CHUNK)]
     remote(part, part, xs.at[0], xo.at[0], rep_dev).wait_send()
     w_send.wait_send()
     for copy in (*core_copies.values(), *y_copies.values()):
@@ -298,7 +313,7 @@
 
     def local(adj_tiles, tile_rows, tile_cols, tile_counts, features_t, weight, bias_vec, cotangent):
         width, block = features_t.shape
-        half_w, half_b = width // 2, block // 2
+        half_b = block // 2
         out_w = weight.shape[1]
         nodes = cotangent.shape[0]
         vmem = pl.BlockSpec(memory_space=pltpu.VMEM)
@@ -322,13 +337,15 @@
                 pltpu.VMEM((4, block, block), F32),
                 pltpu.VMEM((4, block, block), BF16),
                 pltpu.VMEM((4, block, block), BF16),
-                pltpu.VMEM((4, 2, width, half_b), F32),
+                pltpu.VMEM((2, 4, width, half_b), F32),
                 pltpu.VMEM((2, 4, width, half_b), F32),
                 pltpu.VMEM((2, 4, width, half_b), F32),
                 pltpu.VMEM((2, 4, width, half_b), F32),
                 pltpu.VMEM((2, 4, width, half_b), F32),
                 pltpu.VMEM((2 * width, half_b), F32),
                 pltpu.VMEM((2 * width, out_w), F32),
+                pltpu.VMEM((6 * width, out_w), BF16),
+                pltpu.VMEM((4, 2 * width, block), BF16),
                 pltpu.VMEM((nodes, out_w), F32),
                 pltpu.VMEM((nodes, out_w), F32),
                 pltpu.VMEM((PIECES, 5, out_w), F32),

time: 81.6 us -> 80.6 us (0.988)
  Pallas kernels: 80.2 us -> 79.2 us
    pallas_call x1, Pallas kernels: 78.6 us -> 77.6 us  [local(): pl.pallas_call(functools.partial(kernel, nz), out_shape=(jax.ShapeDtypeSt...]
where the time goes in v4:
time: 80.6 us; the launch traced here: 80.5 us
  Pallas kernels  79.2 us (98%)
  between operations  1.29 us (2%)
    pallas_call x1, Pallas kernels, local(): pl.pallas_call(functools.partial(kernel, nz), out_shape=(jax.ShapeDtypeSt...  77.6 us

profile of v4, /device:TPU:1, one launch (start us, length us, event | category | flops | bytes accessed | tf_op | source)
XLA Modules:
  0.0 80.5 jit_solution(7190018239220231166)
XLA Ops:
  1.3 77.6 %shard_map.103 = (f32[256,128]{1,0:T(8,128)}, f32[64,128]{1,0:T(8,128)}, f32[1,128]{1,0:T(1,128)}) custom-call(s32[1,1,4]{2,1,0:T(1,128)} %rows_ref.1, s32[1,1,4]{2,1,0:T(1,128)} %cols_ref.1, s32[1,1]{1,0:T(1,128)S(6)} %copy.11.counts_ref, f32[1,1,4,512,512]{4,3,2,1,0:T(8,128)} %adj_ref.1, f32[64,512]{1,0:T(8,128)} %feat_ref.1, f32[64,128]{1,0:T(8,128)} %weight_ref.1, ...), custom_call_target="tpu_custom_call" | custom-call | tf_op jit(solution)/shard_map/pallas_call | solution.py:322
  78.9 1.6 %shard_map.104 = (f32[256,128]{1,0:T(8,128)}, f32[64,128]{1,0:T(8,128)}, f32[1,128]{1,0:T(1,128)}) custom-call(f32[256,128]{1,0:T(8,128)} %get-tuple-element.9.output, f32[64,128]{1,0:T(8,128)} %get-tuple-element.10.grad_weight, f32[1,128]{1,0:T(1,128)} %get-tuple-element.11.grad_bias), custom_call_target="tpu_custom_call" | custom-call | tf_op jit(solution)/shard_map/pallas_call | solution.py:374

commit v5 on v4

--- a/solution.py
+++ b/solution.py
@@ -13,6 +13,7 @@
 
 NY = 4
 PIECES = 32
+FAR_FIRST = (2, 1, 3, 0)
 CHUNK = 16
 OWN_ORDER = (2, 0, 1, 3)
 X_COUNT = (3, 3, 3, 3, 3, 2, 2)
@@ -36,7 +37,7 @@
     out_ref, gw_ref, gb_ref,
     rows_at, cols, counts, bias, gath, adj_in, adj_hi, adj_lo, prod, m_out, c1_in, s_buf,
     y_in, mt, w_full, w_three, x_both, cot, out_v,
-    g_buf, f1_in, f2_in, f3_in, p2, p3,
+    g_buf, f1_in, f2_in, p2, p3, bias_v,
     zr, xr, xo, zs, xs, lsem, asem, wsem, csem, ysem, fsem, ready,
 ):
     row, col, rep = lax.axis_index("row"), lax.axis_index("col"), lax.axis_index("rep")
@@ -201,13 +202,20 @@
         high, low = halves(gath[jnp.clip(cols[0, 0, t], 0, 2 * nz - 1)])
         x_both[t] = jnp.concatenate([high, low], axis=0)
 
-    def placed(group, n):
-        total = None
-        for t in range(4):
-            scale = jnp.where((t < count) & (rows_at[0, 0, t] == group), F32(1.0), F32(0.0))
-            term = prod[n, t] * scale
-            total = term if total is None else total + term
-        return total
+    def placed(side, n):
+        scales = {
+            k: [
+                jnp.where((t < count) & (rows_at[0, 0, t] == ((y + k) % NY) * 2 + side), F32(1.0), F32(0.0))
+                for t in range(4)
+            ]
+            for k in FAR_FIRST
+        }
+        for low in (0, width // 2):
+            rows = pl.ds(low, width // 2)
+            values = [prod[n, t, rows, :] for t in range(4)]
+            for k in FAR_FIRST:
+                terms = [value * scale for value, scale in zip(values, scales[k])]
+                yield k, rows, low > 0, (terms[0] + terms[1]) + (terms[2] + terms[3])
 
     core_copies = {}
     for n, h in order:
@@ -217,17 +225,19 @@
             both = lax.dot_general(x_both[t], adj_hi[t, nodes, :], dims, preferred_element_type=F32)
             rest = lax.dot_general(x_both[t, 0:width], adj_lo[t, nodes, :], dims, preferred_element_type=F32)
             prod[n, t] = both[:width] + both[width:] + rest
-        for k in (2, 1, 3, 0):
-            m_out[n, k] = placed(((y + k) % NY) * 2 + 1 - core, n)
-            copy = remote(m_out.at[n, k], c1_in.at[n, k], csem.at[0, n, k], csem.at[1, n, k], core_dev)
-            copy.start()
-            core_copies[n, k] = copy
+        for k, rows, whole, total in placed(1 - core, n):
+            m_out[n, k, rows, :] = total
+            if whole:
+                copy = remote(m_out.at[n, k], c1_in.at[n, k], csem.at[0, n, k], csem.at[1, n, k], core_dev)
+                copy.start()
+                core_copies[n, k] = copy
+        for k, rows, _, total in placed(core, n):
+            s_buf[n, k, rows, :] = total
 
     y_copies = {}
     for n, k in SENDING:
-        total = placed(((y + k) % NY) * 2 + core, n)
         core_copies[n, k].wait_recv()
-        s_buf[n, k] = total + c1_in[n, k]
+        s_buf[n, k] += c1_in[n, k]
         if (n, k) != (1, 0):
             device = {"col": ((y + k) % NY) * 2 + core, "rep": order[n][1]}
             copy = remote(s_buf.at[n, k], y_in.at[n, k], ysem.at[0, n, k], ysem.at[1, n, k], device)
@@ -276,19 +286,21 @@
     mine = jnp.sum(f2_in[...], axis=0)
     p3[...] = mine[0:4]
     here = x_lo * 8 + col
-    f3_in[here] = mine[0:4]
+    own_out = pltpu.make_async_copy(p3, gw_ref.at[here], lsem.at[8])
     for i in (1, 0):
         for j in (4, 3, 5, 2, 6, 1, 7, 0):
             if i + j > 0:
                 device = {"row": (x_lo + i - 2 * i * x_lo) * nz + z, "col": cols_of[j]}
-                remote(p3, f3_in.at[here], fsem.at[4], fsem.at[5], device).start()
-    gb_ref[...] = mine[4:5]
-    f3_others = f3_in.at[pl.ds(0, 15)]
+                remote(p3, gw_ref.at[here], fsem.at[4], fsem.at[5], device).start()
+    own_out.start()
+    bias_v[...] = mine[4:5]
+    bias_out = pltpu.make_async_copy(bias_v, gb_ref, lsem.at[9])
+    bias_out.start()
+    f3_others = gw_ref.at[pl.ds(0, 15)]
     remote(f3_others, f3_others, fsem.at[4], fsem.at[5], rep_dev).wait()
-    for k in range(16):
-        gw_ref[4 * k : 4 * k + 4, :] = f3_in[k]
-
-    out_copy.wait()
+
+    for copy in (out_copy, own_out, bias_out):
+        copy.wait()
     part = gath.at[pl.ds(0, nz - 1)]
     remote(part, part, zs.at[0], xo.at[0], rep_dev).wait_send()
     part = gath.at[pl.ds(0, sum(4 - c for c in X_COUNT) + 2), pl.ds(0, 2 * CHUNK)]
@@ -304,7 +316,8 @@
 
 def hand_over(output, grad_weight, grad_bias, out_ref, gw_ref, gb_ref):
     out_ref[...] = output[...]
-    gw_ref[...] = grad_weight[...]
+    for k in range(16):
+        gw_ref[4 * k : 4 * k + 4, :] = grad_weight[k]
     gb_ref[...] = grad_bias[...]
 
 
@@ -323,11 +336,11 @@
             functools.partial(kernel, nz),
             out_shape=(
                 jax.ShapeDtypeStruct((nodes, out_w), F32),
-                jax.ShapeDtypeStruct((width, out_w), F32),
+                jax.ShapeDtypeStruct((16, width // 16, out_w), F32),
                 jax.ShapeDtypeStruct((1, out_w), F32),
             ),
             in_specs=[hbm] * 8,
-            out_specs=(hbm, vmem, vmem),
+            out_specs=(hbm,) * 3,
             scratch_shapes=[
                 pltpu.SMEM(tile_rows.shape, jnp.int32),
                 pltpu.SMEM(tile_cols.shape, jnp.int32),
@@ -351,15 +364,15 @@
                 pltpu.VMEM((PIECES, 5, out_w), F32),
                 pltpu.VMEM((PIECES - 1, 5, out_w), F32),
                 pltpu.VMEM((nz, 5, out_w), F32),
-                pltpu.VMEM((16, 4, out_w), F32),
                 pltpu.VMEM((5, out_w), F32),
                 pltpu.VMEM((4, out_w), F32),
+                pltpu.VMEM((1, out_w), F32),
                 dma((2, nz // 2, 6)),
                 dma((2, nz // 2 - 1, 3)),
                 dma((4,)),
                 dma((2,)),
                 dma((1,)),
-                dma((8,)),
+                dma((10,)),
                 dma((4,)),
                 dma((2,)),
                 dma((2, 2, 4)),
@@ -373,7 +386,9 @@
         )(tile_rows, tile_cols, tile_counts, adj_tiles, features_t, weight, bias_vec.reshape(1, out_w), cotangent)
         output, grad_weight, grad_bias = pl.pallas_call(
             hand_over,
-            out_shape=tuple(jax.ShapeDtypeStruct(a.shape, F32) for a in (output, grad_weight, grad_bias)),
+            out_shape=tuple(
+                jax.ShapeDtypeStruct(shape, F32) for shape in (output.shape, (width, out_w), grad_bias.shape)
+            ),
             in_specs=[vmem] * 3,
             out_specs=(vmem,) * 3,
         )(output, grad_weight, grad_bias)

time: 80.6 us -> 79.9 us (level)
  no operation moved by 1% of the time
where the time goes in v5:
time: 79.9 us; the launch traced here: 79.7 us
  Pallas kernels  78.4 us (98%)
  between operations  1.29 us (2%)
    pallas_call x1, Pallas kernels, local(): pl.pallas_call(functools.partial(kernel, nz), out_shape=(jax.ShapeDtypeSt...  76.8 us

profile of v5, /device:TPU:1, one launch (start us, length us, event | category | flops | bytes accessed | tf_op | source)
XLA Modules:
  0.0 79.7 jit_solution(304610343643803632)
XLA Ops:
  1.3 76.8 %shard_map.103 = (f32[256,128]{1,0:T(8,128)}, f32[16,4,128]{2,1,0:T(4,128)}, f32[1,128]{1,0:T(1,128)}) custom-call(s32[1,1,4]{2,1,0:T(1,128)} %rows_ref.1, s32[1,1,4]{2,1,0:T(1,128)} %cols_ref.1, s32[1,1]{1,0:T(1,128)S(6)} %copy.11.counts_ref, f32[1,1,4,512,512]{4,3,2,1,0:T(8,128)} %adj_ref.1, f32[64,512]{1,0:T(8,128)} %feat_ref.1, f32[64,128]{1,0:T(8,128)} %weight_ref.1, ...), custom_call_target="tpu_custom_call" | custom-call | tf_op jit(solution)/shard_map/pallas_call | solution.py:335
  78.1 1.6 %shard_map.104 = (f32[256,128]{1,0:T(8,128)}, f32[64,128]{1,0:T(8,128)}, f32[1,128]{1,0:T(1,128)}) custom-call(f32[256,128]{1,0:T(8,128)} %get-tuple-element.9.output, f32[16,4,128]{2,1,0:T(4,128)} %get-tuple-element.10.grad_weight, f32[1,128]{1,0:T(1,128)} %get-tuple-element.11.grad_bias), custom_call_target="tpu_custom_call" | custom-call | tf_op jit(solution)/shard_map/pallas_call | solution.py:387

commit v6 on v5

--- a/solution.py
+++ b/solution.py
@@ -17,7 +17,7 @@
 CHUNK = 16
 OWN_ORDER = (2, 0, 1, 3)
 X_COUNT = (3, 3, 3, 3, 3, 2, 2)
-SENDING = ((0, 2), (0, 1), (0, 3), (0, 0), (1, 2), (1, 1), (1, 3), (1, 0))
+SENDING = ((0, 2), (0, 1), (0, 3), (1, 2), (0, 0), (1, 1), (1, 3), (1, 0))
 
 
 def remote(src, dst, send_sem, recv_sem, device):
@@ -314,11 +314,22 @@
     remote(others, others, fsem.at[2], fsem.at[3], rep_dev).wait_send()
 
 
-def hand_over(output, grad_weight, grad_bias, out_ref, gw_ref, gb_ref):
-    out_ref[...] = output[...]
+def hand_over(output, grad_weight, grad_bias, out_ref, gw_ref, gb_ref, out_v, gw_in, gw_v, gb_v, sems):
+    pairs = ((grad_weight, gw_in), (output, out_v), (grad_bias, gb_v))
+    copies = [pltpu.make_async_copy(source, place, sems.at[0, k]) for k, (source, place) in enumerate(pairs)]
+    pairs = ((gw_v, gw_ref), (out_v, out_ref), (gb_v, gb_ref))
+    stores = [pltpu.make_async_copy(source, place, sems.at[1, k]) for k, (source, place) in enumerate(pairs)]
+    for copy in copies:
+        copy.start()
+    for k in (1, 2):
+        copies[k].wait()
+        stores[k].start()
+    copies[0].wait()
     for k in range(16):
-        gw_ref[4 * k : 4 * k + 4, :] = grad_weight[k]
-    gb_ref[...] = grad_bias[...]
+        gw_v[4 * k : 4 * k + 4, :] = gw_in[k]
+    stores[0].start()
+    for store in stores:
+        store.wait()
 
 
 def solution(mesh):
@@ -329,7 +340,6 @@
         half_b = block // 2
         out_w = weight.shape[1]
         nodes = cotangent.shape[0]
-        vmem = pl.BlockSpec(memory_space=pltpu.VMEM)
         hbm = pl.BlockSpec(memory_space=pltpu.HBM)
         dma = pltpu.SemaphoreType.DMA
         output, grad_weight, grad_bias = pl.pallas_call(
@@ -389,8 +399,16 @@
             out_shape=tuple(
                 jax.ShapeDtypeStruct(shape, F32) for shape in (output.shape, (width, out_w), grad_bias.shape)
             ),
-            in_specs=[vmem] * 3,
-            out_specs=(vmem,) * 3,
+            in_specs=[hbm] * 3,
+            out_specs=(hbm,) * 3,
+            scratch_shapes=[
+                pltpu.VMEM(output.shape, F32),
+                pltpu.VMEM(grad_weight.shape, F32),
+                pltpu.VMEM((width, out_w), F32),
+                pltpu.VMEM(grad_bias.shape, F32),
+                dma((2, 3)),
+            ],
+            compiler_params=pltpu.CompilerParams(vmem_limit_bytes=67043328),
         )(output, grad_weight, grad_bias)
         return output, grad_weight, grad_bias.reshape(out_w)
 

time: 79.9 us -> 79.9 us (level)
  no operation moved by 1% of the time
where the time goes in v6:
time: 79.9 us; the launch traced here: 79.8 us
  Pallas kernels  78.5 us (98%)
  between operations  1.29 us (2%)
    pallas_call x1, Pallas kernels, local(): pl.pallas_call(functools.partial(kernel, nz), out_shape=(jax.ShapeDtypeSt...  76.8 us
    pallas_call x1, Pallas kernels, local(): pl.pallas_call(hand_over, out_shape=tuple((jax.ShapeDtypeStruct(shape, F3...  1.64 us

profile of v6, /device:TPU:1, one launch (start us, length us, event | category | flops | bytes accessed | tf_op | source)
XLA Modules:
  0.0 79.8 jit_solution(18319692459808421949)
XLA Ops:
  1.3 76.8 %shard_map.103 = (f32[256,128]{1,0:T(8,128)}, f32[16,4,128]{2,1,0:T(4,128)}, f32[1,128]{1,0:T(1,128)}) custom-call(s32[1,1,4]{2,1,0:T(1,128)} %rows_ref.1, s32[1,1,4]{2,1,0:T(1,128)} %cols_ref.1, s32[1,1]{1,0:T(1,128)S(6)} %copy.11.counts_ref, f32[1,1,4,512,512]{4,3,2,1,0:T(8,128)} %adj_ref.1, f32[64,512]{1,0:T(8,128)} %feat_ref.1, f32[64,128]{1,0:T(8,128)} %weight_ref.1, ...), custom_call_target="tpu_custom_call" | custom-call | tf_op jit(solution)/shard_map/pallas_call | solution.py:345
  78.1 1.6 %shard_map.104 = (f32[256,128]{1,0:T(8,128)}, f32[64,128]{1,0:T(8,128)}, f32[1,128]{1,0:T(1,128)}) custom-call(f32[256,128]{1,0:T(8,128)} %get-tuple-element.9.output, f32[16,4,128]{2,1,0:T(4,128)} %get-tuple-element.10.grad_weight, f32[1,128]{1,0:T(1,128)} %get-tuple-element.11.grad_bias), custom_call_target="tpu_custom_call" | custom-call | tf_op jit(solution)/shard_map/pallas_call | solution.py:397

commit v7 on v5

--- a/solution.py
+++ b/solution.py
@@ -198,9 +198,6 @@
 
     count = counts[0, 0]
     order = ((0, 1 - rep), (1, rep))
-    for t in range(4):
-        high, low = halves(gath[jnp.clip(cols[0, 0, t], 0, 2 * nz - 1)])
-        x_both[t] = jnp.concatenate([high, low], axis=0)
 
     def placed(side, n):
         scales = {
@@ -222,6 +219,9 @@
         for t in range(4):
             nodes = pl.ds(pl.multiple_of(h * half_b, half_b), half_b)
             dims = (((1,), (1,)), ((), ()))
+            if n == 0:
+                high, low = halves(gath[jnp.clip(cols[0, 0, t], 0, 2 * nz - 1)])
+                x_both[t] = jnp.concatenate([high, low], axis=0)
             both = lax.dot_general(x_both[t], adj_hi[t, nodes, :], dims, preferred_element_type=F32)
             rest = lax.dot_general(x_both[t, 0:width], adj_lo[t, nodes, :], dims, preferred_element_type=F32)
             prod[n, t] = both[:width] + both[width:] + rest

time: 79.9 us -> 79.9 us (level)
  no operation moved by 1% of the time
where the time goes in v7:
time: 79.9 us; the launch traced here: 79.7 us
  Pallas kernels  78.4 us (98%)
  between operations  1.29 us (2%)
    pallas_call x1, Pallas kernels, local(): pl.pallas_call(functools.partial(kernel, nz), out_shape=(jax.ShapeDtypeSt...  76.8 us

profile of v7, /device:TPU:1, one launch (start us, length us, event | category | flops | bytes accessed | tf_op | source)
XLA Modules:
  0.0 79.7 jit_solution(304610343643803632)
XLA Ops:
  1.3 76.8 %shard_map.103 = (f32[256,128]{1,0:T(8,128)}, f32[16,4,128]{2,1,0:T(4,128)}, f32[1,128]{1,0:T(1,128)}) custom-call(s32[1,1,4]{2,1,0:T(1,128)} %rows_ref.1, s32[1,1,4]{2,1,0:T(1,128)} %cols_ref.1, s32[1,1]{1,0:T(1,128)S(6)} %copy.11.counts_ref, f32[1,1,4,512,512]{4,3,2,1,0:T(8,128)} %adj_ref.1, f32[64,512]{1,0:T(8,128)} %feat_ref.1, f32[64,128]{1,0:T(8,128)} %weight_ref.1, ...), custom_call_target="tpu_custom_call" | custom-call | tf_op jit(solution)/shard_map/pallas_call | solution.py:335
  78.1 1.6 %shard_map.104 = (f32[256,128]{1,0:T(8,128)}, f32[64,128]{1,0:T(8,128)}, f32[1,128]{1,0:T(1,128)}) custom-call(f32[256,128]{1,0:T(8,128)} %get-tuple-element.9.output, f32[16,4,128]{2,1,0:T(4,128)} %get-tuple-element.10.grad_weight, f32[1,128]{1,0:T(1,128)} %get-tuple-element.11.grad_bias), custom_call_target="tpu_custom_call" | custom-call | tf_op jit(solution)/shard_map/pallas_call | solution.py:387
